TPU v7x, 32 devices: a whole 2x2x4 slice. The times are simulated.
32 devices in a mesh: wide: 16 (over z, x, core), narrow: 2 (over y).
Axes of the slice: x: 2, y: 2, z: 4, core: 2. Of those that a mesh axis runs over, the one named last changes fastest.
Arguments:
- tokens: bfloat16 [32, 16384], P('wide', 'narrow'), may hold values from -6 to 6
- q_weight: bfloat16 [16384, 16384], P('narrow', 'wide'), may hold values from -0.046875 to 0.046875
- key_value_weight: bfloat16 [16384, 2048], P('narrow', 'wide'), may hold values from -0.046875 to 0.046875
- out_weight: bfloat16 [16384, 16384], P('narrow', 'wide'), may hold values from -0.046875 to 0.046875
- stored_keys: bfloat16 [32, 256, 1024], P(('wide', 'narrow')), may hold values from -6 to 6
- stored_values: bfloat16 [32, 256, 1024], P(('wide', 'narrow')), may hold values from -6 to 6
- channel_key_scale: float32 [32, 1024], P(('wide', 'narrow')), may hold values from 0.5 to 64
- lengths: int32 [32], P(('wide', 'narrow')), may hold values from 1 to 256, 4096 in all
Outputs:
- attn_out: bfloat16 [32, 16384], P('narrow', 'wide')
Inputs may be any that keep to these rules, and one draw needn't show every extreme that they name: `lengths`: each request holds 1 to 256 cached tokens, and some request holds exactly 256.
All inputs are finite; a program needn't handle non-finite values. No bound on the sum of `lengths` on one device may be relied on, other than what follows from the above.
Results may differ from a plain program's by a relative error of at most 0.005.
The roundings to bfloat16 on the way count: a program that leaves them out, or rounds other values in their place, can miss the bound.
Values may be sent and summed in bfloat16 or wider, within the bound.
No kernel may reach another device: no remote copies, remote signals or barrier semaphores. Data moves between devices by JAX's collectives and lax.ppermute only.
A program may use at most 128 MiB of HBM per device.

v0:
```python
import math

import jax
import jax.numpy as jnp
from jax import lax
from jax.sharding import PartitionSpec as P

QUERY_HEADS = 128
KEY_VALUE_HEADS = 8
HEAD_SIZE = 128


def apply_rotation(values, token_position):
    half = values.shape[-1] // 2
    freq = jnp.exp(jnp.arange(half, dtype=jnp.float32) * (-2.0 * math.log(500000.0) / HEAD_SIZE))
    angle = token_position * freq
    cosine = jnp.cos(angle)
    sine = jnp.sin(angle)
    first = values[..., :half]
    second = values[..., half:]
    return jnp.concatenate(
        [first * cosine - second * sine, second * cosine + first * sine], axis=-1
    )


def attend(query_vector, current_token, stored_keys, stored_values, channel_key_scale, lengths):
    owning_devices = query_vector.shape[0]
    slot_indices = stored_keys.shape[1]
    group_index = QUERY_HEADS // KEY_VALUE_HEADS
    inverse_scale = HEAD_SIZE ** (-0.5)
    token_position = lengths.astype(jnp.float32)
    rotated_query = apply_rotation(
        query_vector.astype(jnp.float32).reshape(
            owning_devices, KEY_VALUE_HEADS, group_index, HEAD_SIZE
        ),
        token_position[:, None, None, None],
    )
    rotated_key = apply_rotation(
        current_token[:, : KEY_VALUE_HEADS * HEAD_SIZE]
        .astype(jnp.float32)
        .reshape(owning_devices, KEY_VALUE_HEADS, HEAD_SIZE),
        token_position[:, None, None],
    )
    current_value = current_token[:, KEY_VALUE_HEADS * HEAD_SIZE :].reshape(
        owning_devices, KEY_VALUE_HEADS, HEAD_SIZE
    )
    stored_query = (
        rotated_query
        * channel_key_scale.reshape(owning_devices, KEY_VALUE_HEADS, 1, HEAD_SIZE)
        * inverse_scale
    ).astype(jnp.bfloat16)
    fresh_query = (rotated_query * inverse_scale).astype(jnp.bfloat16)
    fresh_key = rotated_key.astype(jnp.bfloat16)
    keys_divided = stored_keys.reshape(owning_devices, slot_indices, KEY_VALUE_HEADS, HEAD_SIZE)
    values_divided = stored_values.reshape(owning_devices, slot_indices, KEY_VALUE_HEADS, HEAD_SIZE)
    scores = jnp.einsum(
        "rgic,rpgc->rgip", stored_query, keys_divided, preferred_element_type=jnp.float32
    )
    fresh_score = jnp.sum(
        fresh_query.astype(jnp.float32) * fresh_key.astype(jnp.float32)[:, :, None, :], axis=-1
    )
    valid = (
        jnp.arange(slot_indices, dtype=jnp.int32)[None, None, None, :]
        < lengths[:, None, None, None]
    )
    masked = jnp.where(valid, scores, jnp.float32(-1e30))
    top = jnp.maximum(jnp.max(masked, axis=-1), fresh_score)
    exps = jnp.where(valid, jnp.exp(masked - top[..., None]), jnp.float32(0.0))
    fresh_exp = jnp.exp(fresh_score - top)
    total = jnp.sum(exps, axis=-1) + fresh_exp
    weights = exps.astype(jnp.bfloat16)
    fresh_weight = fresh_exp.astype(jnp.bfloat16)
    summed = jnp.einsum(
        "rgip,rpgc->rgic", weights, values_divided, preferred_element_type=jnp.float32
    )
    summed = (
        summed
        + fresh_weight.astype(jnp.float32)[..., None]
        * current_value.astype(jnp.float32)[:, :, None, :]
    )
    return (
        (summed / total[..., None])
        .astype(jnp.bfloat16)
        .reshape(owning_devices, QUERY_HEADS * HEAD_SIZE)
    )


def body(
    tokens,
    q_weight,
    key_value_weight,
    out_weight,
    stored_keys,
    stored_values,
    channel_key_scale,
    lengths,
):
    wide_count = lax.axis_size("wide")
    narrow = lax.axis_size("narrow")
    query_cols = q_weight.shape[1]
    row_width = query_cols + key_value_weight.shape[1]
    per_owner = stored_keys.shape[0]
    piece = lax.all_gather(tokens, "wide", axis=0, tiled=True)
    partial_terms = jnp.concatenate(
        [
            jnp.dot(piece, q_weight, preferred_element_type=jnp.float32),
            jnp.dot(piece, key_value_weight, preferred_element_type=jnp.float32),
        ],
        axis=1,
    )
    grouped = partial_terms.reshape(wide_count, narrow, per_owner, row_width).transpose(1, 0, 2, 3)
    grouped = grouped.reshape(narrow * wide_count * per_owner, row_width)
    summed = lax.psum_scatter(grouped, "narrow", scatter_dimension=0, tiled=True).astype(
        jnp.bfloat16
    )
    owned = lax.all_to_all(summed, "wide", split_axis=0, concat_axis=1, tiled=True)
    owned = owned.reshape(per_owner, wide_count, row_width)
    query_vector = owned[:, :, :query_cols].reshape(per_owner, wide_count * query_cols)
    current_token = owned[:, :, query_cols:].reshape(
        per_owner, wide_count * (row_width - query_cols)
    )
    attended = attend(
        query_vector, current_token, stored_keys, stored_values, channel_key_scale, lengths
    )
    peers = lax.all_gather(attended, "wide", axis=0, tiled=True)
    owners_rows = lax.all_to_all(peers, "narrow", split_axis=1, concat_axis=0, tiled=True)
    ordered = owners_rows.reshape(narrow, wide_count, per_owner, out_weight.shape[0]).transpose(
        1, 0, 2, 3
    )
    ordered = ordered.reshape(narrow * wide_count * per_owner, out_weight.shape[0])
    terms = jnp.dot(ordered, out_weight, preferred_element_type=jnp.float32)
    return lax.psum_scatter(terms, "narrow", scatter_dimension=0, tiled=True).astype(jnp.bfloat16)


def solution(mesh):
    placed = (
        P("wide", "narrow"),
        P("narrow", "wide"),
        P("narrow", "wide"),
        P("narrow", "wide"),
        P(("wide", "narrow"), None, None),
        P(("wide", "narrow"), None, None),
        P(("wide", "narrow"), None),
        P(("wide", "narrow")),
    )
    return jax.shard_map(
        body, mesh=mesh, in_specs=placed, out_specs=P("narrow", "wide"), check_vma=False
    )
```

profile of v0, /device:TPU:0, one launch (start us, length us, event | category | flops | bytes accessed | tf_op | source)
XLA Modules:
  0.0 129.3 jit_solution(10535297823184384475)
XLA Ops:
  6.5 0.0 copy-start
  6.5 0.0 reduce-scatter.3.cloned.1.call-start
  6.5 0.0 copy-start.2
  6.5 24.9 %all-gather = bf16[16,2,8192]{2,1,0:T(2,128)(2,1)S(1)} all-gather(bf16[1,2,8192]{2,1,0:T(2,128)(2,1)} %bitcast.62), channel_id=1, replica_groups=mesh['wide'=16,'narrow'=2] {'wide'}, dimensions={0}, use_global_device_ids=true | all-gather | bytes 557056 | tf_op jit(solution)/shard_map/all_gather | solution.py:103
  31.5 0.2 reshape.292
  31.7 0.0 copy-done
  31.7 0.0 copy-start.1
  31.7 0.4 fusion.26
  32.1 8.7 %fusion.25 = f32[32,1024]{1,0:T(8,128)S(1)} fusion(bf16[32,8192]{1,0:T(8,128)(2,1)S(1)} %reshape.292, bf16[8192,1024]{1,0:T(8,128)(2,1)} %param.9), kind=kOutput, calls=%fused_computation.47 | convolution fusion | flops 536870912 | bytes 17432576 | tf_op jit(solution)/shard_map/dot_general | solution.py:106
  40.9 0.1 reshape.276
  41.0 0.7 copy.20
  41.7 0.0 reduce-scatter.3.cloned.1.call-update
  42.3 0.0 copy-done.1
  42.4 0.1 copy.28
  42.5 1.1 copy.30
  43.6 0.1 fusion.19
  43.7 6.0 %reduce-scatter.3.cloned.1.call-done = f32[16,1152]{1,0:T(8,128)} async-done(((f32[32,1152]{1,0:T(8,128)}), f32[16,1152]{1,0:T(8,128)}) %reduce-scatter.3.cloned.1.call-update) | async-done | bytes 73744 | tf_op jit(solution)/shard_map/reduce_scatter | solution.py:113
  49.7 0.9 convert_bitcast_fusion
  50.5 0.5 broadcast.103
  51.1 0.7 reduce.6
  51.7 0.7 reshape.299
  52.4 5.6 %all-to-all-start = ((bf16[16,2,576]{2,1,0:T(2,128)(2,1)}), bf16[16,2,576]{2,1,0:T(2,128)(2,1)S(1)}, u32[]{:S(2)}, u32[]{:S(2)}) async-start(bf16[16,2,576]{2,1,0:T(2,128)(2,1)} %reshape.299), calls=%async_computation.1 | async-start | bytes 81920 | tf_op jit(solution)/shard_map/all_to_all | solution.py:116
  58.1 0.0 reduce-scatter.5.cloned.1.call-start
  58.1 6.6 %all-to-all-done = bf16[16,2,576]{2,1,0:T(2,128)(2,1)S(1)} async-done(((bf16[16,2,576]{2,1,0:T(2,128)(2,1)}), bf16[16,2,576]{2,1,0:T(2,128)(2,1)S(1)}, u32[]{:S(2)}, u32[]{:S(2)}) %all-to-all-start) | async-done | bytes 36896 | tf_op jit(solution)/shard_map/all_to_all | solution.py:116
  64.8 0.1 reshape.300
  65.0 0.1 fusion.16
  65.1 0.1 multiply_subtract_fusion
  65.2 0.1 maximum_convert_fusion
  65.2 0.2 multiply_reduce_fusion
  65.4 0.0 copy-done.2
  65.4 0.4 fusion.24
  65.8 0.2 fusion.4
  66.0 0.2 fusion.1
  66.3 20.7 %all-gather.1 = bf16[16,1,16384]{2,1,0:T(2,128)(2,1)S(1)} all-gather(bf16[1,1,16384]{2,1,0:T(2,128)(2,1)S(1)} %reshape.293), channel_id=1, replica_groups=mesh['wide'=16,'narrow'=2] {'wide'}, dimensions={0}, use_global_device_ids=true | all-gather | bytes 557056 | tf_op jit(solution)/shard_map/all_gather | solution.py:125
  87.0 3.9 %reduce.5 = bf16[16,16384]{1,0:T(8,128)(2,1)} reduce(bf16[16,1,16384]{2,1,0:T(2,128)(2,1)S(1)} %all-gather.1, bf16[]{:T(256)} %constant.15), dimensions={1}, to_apply=%all-gather.1.reduce_sub_computation | reduce | bytes 1048578 | tf_op jit(solution)/shard_map/all_gather | solution.py:125
  90.9 1.1 copy.40
  92.0 11.2 %all_to_all.29 = bf16[16,2,8192]{2,0,1:T(8,128)(2,1)S(1)} all-to-all(bf16[16,2,8192]{2,0,1:T(8,128)(2,1)S(1)} %bitcast.51), channel_id=1, replica_groups=mesh['wide'=16,'narrow'=2] {'narrow'}, dimensions={1} | all-to-all | bytes 1048576 | tf_op jit(solution)/shard_map/all_to_all | solution.py:126
  103.2 0.5 copy.25
  103.7 0.2 reshape.286
  103.9 9.4 %fusion.27 = f32[32,1024]{1,0:T(8,128)} fusion(bf16[32,8192]{1,0:T(8,128)(2,1)S(1)} %reshape.286, bf16[8192,1024]{1,0:T(8,128)(2,1)} %param.11), kind=kOutput, calls=%fused_computation.49 | convolution fusion | flops 536870912 | bytes 17432576 | tf_op jit(solution)/shard_map/dot_general | solution.py:131
  113.3 0.0 reduce-scatter.5.cloned.1.call-update
  113.4 7.7 %reduce-scatter.5.cloned.1.call-done = f32[16,1024]{1,0:T(8,128)} async-done(((f32[32,1024]{1,0:T(8,128)}), f32[16,1024]{1,0:T(8,128)}) %reduce-scatter.5.cloned.1.call-update) | async-done | bytes 65552 | tf_op jit(solution)/shard_map/reduce_scatter | solution.py:132
  121.0 1.5 %convert_element_type.121 = bf16[16,1024]{1,0:T(8,128)(2,1)} convert(f32[16,1024]{1,0:T(8,128)} %reduce-scatter.5.cloned.1.call-done) | non-fusion elementwise | flops 16384 | bytes 98304 | tf_op jit(solution)/shard_map/convert_element_type | solution.py:132
  (11 shorter events, 0.1 us)
Async XLA Ops:
  6.5 25.1 %copy-start = (bf16[8192,128]{1,0:T(8,128)(2,1)S(1)}, bf16[8192,128]{1,0:T(8,128)(2,1)}, u32[]{:S(2)}) copy-start(bf16[8192,128]{1,0:T(8,128)(2,1)} %param.10) | copy-start | bytes 6291460
  6.5 43.1 %reduce-scatter.3.cloned.1.call-start = ((), (), s32[]{:S(2)}) async-start(), calls=%async_computation.4 | async-start | bytes 221184 | tf_op jit(solution)/shard_map/reduce_scatter | solution.py:113
  6.5 58.9 %copy-start.2 = (f32[1,1024]{1,0:T(1,128)S(1)}, f32[1,1024]{1,0:T(1,128)}, u32[]{:S(2)}) copy-start(f32[1,1024]{1,0:T(1,128)} %param.14) | copy-start | bytes 12292
  31.7 10.7 %copy-start.1 = (bf16[1,256,1024]{2,1,0:T(8,128)(2,1)S(1)}, bf16[1,256,1024]{2,1,0:T(8,128)(2,1)}, u32[]{:S(2)}) copy-start(bf16[1,256,1024]{2,1,0:T(8,128)(2,1)} %param.12) | copy-start | bytes 1572868
  52.4 12.3 %all-to-all-start = ((bf16[16,2,576]{2,1,0:T(2,128)(2,1)}), bf16[16,2,576]{2,1,0:T(2,128)(2,1)S(1)}, u32[]{:S(2)}, u32[]{:S(2)}) async-start(bf16[16,2,576]{2,1,0:T(2,128)(2,1)} %reshape.299), calls=%async_computation.1 | async-start | bytes 81920 | tf_op jit(solution)/shard_map/all_to_all | solution.py:116
  58.1 63.0 %reduce-scatter.5.cloned.1.call-start = ((), (), s32[]{:S(2)}) async-start(), calls=%async_computation.5 | async-start | bytes 196608 | tf_op jit(solution)/shard_map/reduce_scatter | solution.py:132
Sparse Core Ops, SparseCore 0:
  41.8 7.7 reduce-scatter.2
  113.5 7.5 reduce-scatter.4
where the time goes:
time: 130 us; the launch traced here: 129 us
  blocking collectives  56.8 us (44%)
  waiting for transfers between devices  20.4 us (16%)
  matrix products  19.2 us (15%)
  between operations  14.3 us (11%)
  other arithmetic  7.64 us (6%)
  starting transfers between devices  5.66 us (4%)
  local copies, waits for them, and re-layouts  5.41 us (4%)
    all_gather x1, blocking collectives, body(): piece = lax.all_gather(tokens, 'wide', axis=0, tiled=True)  24.9 us
    all_gather x1, blocking collectives, body(): peers = lax.all_gather(attended, 'wide', axis=0, tiled=True)  20.7 us
    all_to_all x1, blocking collectives, body(): lax.all_to_all(peers, 'narrow', split_axis=1, concat_axis=0, tiled=True)  11.2 us
    dot_general x1, matrix products, body(): terms = jnp.dot(ordered, out_weight, preferred_element_type=jnp.float32)  9.39 us
    dot_general x1, matrix products, body(): jnp.dot(piece, q_weight, preferred_element_type=jnp.float32)  8.75 us
    reduce_scatter x1, waiting for transfers between devices, body(): lax.psum_scatter(terms, 'narrow', scatter_dimension=0, tiled=True)  7.69 us
    all_to_all x1, waiting for transfers between devices, body(): lax.all_to_all(summed, 'wide', split_axis=0, concat_axis=1, tiled=True)  6.64 us
    reduce_scatter x1, waiting for transfers between devices, body(): lax.psum_scatter(grouped, 'narrow', scatter_dimension=0, tiled=True)  6 us
  transfers between devices with their start and end apart: 3, of which 3 were waited for; matrix products, arithmetic and copies ran while one was open for 1% of the time, Pallas kernels for 0%

commit v1 on v0

--- a/solution.py
+++ b/solution.py
@@ -3,11 +3,15 @@
 import jax
 import jax.numpy as jnp
 from jax import lax
+from jax.sharding import Mesh
 from jax.sharding import PartitionSpec as P
 
 QUERY_HEADS = 128
 KEY_VALUE_HEADS = 8
 HEAD_SIZE = 128
+
+WIDE = ("hi", "lo")
+EVERY = ("hi", "lo", "narrow")
 
 
 def apply_rotation(values, token_position):
@@ -85,6 +89,23 @@
     )
 
 
+def gather_wide(block):
+    count = lax.axis_size(WIDE)
+    me = lax.axis_index(WIDE)
+    held = block
+    depth = 0
+    step = count // 2
+    while step:
+        other = lax.ppermute(held, WIDE, [(i, i ^ step) for i in range(count)])
+        upper = (me & step) != 0
+        held = jnp.stack(
+            [jnp.where(upper, other, held), jnp.where(upper, held, other)], axis=depth
+        )
+        depth += 1
+        step //= 2
+    return held.reshape((count * block.shape[0],) + block.shape[1:])
+
+
 def body(
     tokens,
     q_weight,
@@ -95,12 +116,14 @@
     channel_key_scale,
     lengths,
 ):
-    wide_count = lax.axis_size("wide")
+    high = lax.axis_size("hi")
+    low = lax.axis_size("lo")
+    wide_count = high * low
     narrow = lax.axis_size("narrow")
     query_cols = q_weight.shape[1]
     row_width = query_cols + key_value_weight.shape[1]
     per_owner = stored_keys.shape[0]
-    piece = lax.all_gather(tokens, "wide", axis=0, tiled=True)
+    piece = gather_wide(tokens)
     partial_terms = jnp.concatenate(
         [
             jnp.dot(piece, q_weight, preferred_element_type=jnp.float32),
@@ -108,13 +131,9 @@
         ],
         axis=1,
     )
-    grouped = partial_terms.reshape(wide_count, narrow, per_owner, row_width).transpose(1, 0, 2, 3)
-    grouped = grouped.reshape(narrow * wide_count * per_owner, row_width)
-    summed = lax.psum_scatter(grouped, "narrow", scatter_dimension=0, tiled=True).astype(
-        jnp.bfloat16
-    )
-    owned = lax.all_to_all(summed, "wide", split_axis=0, concat_axis=1, tiled=True)
-    owned = owned.reshape(per_owner, wide_count, row_width)
+    received = lax.all_to_all(partial_terms, EVERY, split_axis=0, concat_axis=0, tiled=True)
+    received = received.reshape(wide_count, narrow, per_owner, row_width)
+    owned = jnp.sum(received, axis=1).astype(jnp.bfloat16).transpose(1, 0, 2)
     query_vector = owned[:, :, :query_cols].reshape(per_owner, wide_count * query_cols)
     current_token = owned[:, :, query_cols:].reshape(
         per_owner, wide_count * (row_width - query_cols)
@@ -122,27 +141,50 @@
     attended = attend(
         query_vector, current_token, stored_keys, stored_values, channel_key_scale, lengths
     )
-    peers = lax.all_gather(attended, "wide", axis=0, tiled=True)
-    owners_rows = lax.all_to_all(peers, "narrow", split_axis=1, concat_axis=0, tiled=True)
-    ordered = owners_rows.reshape(narrow, wide_count, per_owner, out_weight.shape[0]).transpose(
-        1, 0, 2, 3
-    )
-    ordered = ordered.reshape(narrow * wide_count * per_owner, out_weight.shape[0])
+    depth = out_weight.shape[0]
+    parts = attended.reshape(per_owner, narrow, depth).transpose(1, 0, 2)
+    parts = jnp.broadcast_to(parts[None], (high, narrow, per_owner, depth))
+    mine = lax.all_to_all(
+        parts.reshape(high * narrow * per_owner, depth),
+        ("hi", "narrow"),
+        split_axis=0,
+        concat_axis=0,
+        tiled=True,
+    ).reshape(high, 1, narrow * per_owner, depth)
+    ordered = lax.all_gather(mine, "lo", axis=1, tiled=True)
+    ordered = ordered.reshape(wide_count * narrow * per_owner, depth)
     terms = jnp.dot(ordered, out_weight, preferred_element_type=jnp.float32)
-    return lax.psum_scatter(terms, "narrow", scatter_dimension=0, tiled=True).astype(jnp.bfloat16)
+    return sum_narrow(terms).astype(jnp.bfloat16)
+
+
+def sum_narrow(terms):
+    narrow = lax.axis_size("narrow")
+    me = lax.axis_index("narrow")
+    rows = terms.shape[0] // narrow
+    grouped = terms.reshape(narrow, rows, terms.shape[1])
+    total = lax.dynamic_index_in_dim(grouped, me, 0, keepdims=False)
+    for step in range(1, narrow):
+        target = lax.rem(me + step, narrow)
+        leaving = lax.dynamic_index_in_dim(grouped, target, 0, keepdims=False)
+        total = total + lax.ppermute(
+            leaving, "narrow", [(i, (i + step) % narrow) for i in range(narrow)]
+        )
+    return total
 
 
 def solution(mesh):
+    high, low, narrow = mesh.shape["wide"] // 2, 2, mesh.shape["narrow"]
+    fine = Mesh(mesh.devices.reshape(high, low, narrow), EVERY)
     placed = (
-        P("wide", "narrow"),
-        P("narrow", "wide"),
-        P("narrow", "wide"),
-        P("narrow", "wide"),
-        P(("wide", "narrow"), None, None),
-        P(("wide", "narrow"), None, None),
-        P(("wide", "narrow"), None),
-        P(("wide", "narrow")),
+        P(WIDE, "narrow"),
+        P("narrow", WIDE),
+        P("narrow", WIDE),
+        P("narrow", WIDE),
+        P(EVERY, None, None),
+        P(EVERY, None, None),
+        P(EVERY, None),
+        P(EVERY),
     )
     return jax.shard_map(
-        body, mesh=mesh, in_specs=placed, out_specs=P("narrow", "wide"), check_vma=False
+        body, mesh=fine, in_specs=placed, out_specs=P("narrow", WIDE), check_vma=False
     )

time: 130 us -> 85 us (0.65)
  blocking collectives: 56.8 us -> 2.18 us
  between operations: 14.3 us -> 1 us
  starting transfers between devices: 5.66 us -> 18.2 us
  waiting for transfers between devices: 20.4 us -> 29.9 us
    all_gather x2 -> x1, blocking collectives: 45.6 us -> 2.18 us  [body(): ordered = lax.all_gather(mine, 'lo', axis=1, tiled=True)]
    reduce_scatter x2 -> x0, waiting for transfers between devices: 13.7 us -> none  [the longest x1 7.69 us: body(): lax.psum_scatter(terms, 'narrow', scatter_dimension=0, tiled=True)]
    ppermute x0 -> x5, waiting for transfers between devices: none -> 13.4 us  [the longest x4 9.94 us: gather_wide(): other = lax.ppermute(held, WIDE, [(i, i ^ step) for i in range(count)])]
    all_to_all x1 -> x0, blocking collectives: 11.2 us -> none  [body(): lax.all_to_all(peers, 'narrow', split_axis=1, concat_axis=0, tiled=True)]
    all_to_all x1 -> x2, waiting for transfers between devices: 6.64 us -> 16.5 us  [the longest x1 9.59 us: body(): lax.all_to_all(parts.reshape(high * narrow * per_owner, depth), ('hi', 'n...]
    ppermute x0 -> x5, starting transfers between devices: none -> 8.38 us  [the longest x4 7.53 us: gather_wide(): other = lax.ppermute(held, WIDE, [(i, i ^ step) for i in range(count)])]
    all_to_all x1 -> x2, starting transfers between devices: 5.62 us -> 9.78 us  [the longest x1 6.07 us: body(): lax.all_to_all(partial_terms, EVERY, split_axis=0, concat_axis=0, tiled=T...]
    all_gather x1 -> x0, other arithmetic: 3.93 us -> none  [body(): peers = lax.all_gather(attended, 'wide', axis=0, tiled=True)]
  transfers between devices with their start and end apart: 3 -> 7, of which waited for: 3 -> 7; matrix products, arithmetic and copies ran while one was open for 1% -> 2% of each run, Pallas kernels for 0% -> 0%
where the time goes in v1:
time: 85 us; the launch traced here: 84.6 us
  waiting for transfers between devices  29.9 us (35%)
  matrix products  18.6 us (22%)
  starting transfers between devices  18.2 us (21%)
  other arithmetic  8.82 us (10%)
  local copies, waits for them, and re-layouts  5.92 us (7%)
  blocking collectives  2.18 us (3%)
  between operations  1 us (1%)
    ppermute x4, waiting for transfers between devices, gather_wide(): other = lax.ppermute(held, WIDE, [(i, i ^ step) for i in range(count)])  9.94 us
    all_to_all x1, waiting for transfers between devices, body(): lax.all_to_all(parts.reshape(high * narrow * per_owner, depth), ('hi', 'n...  9.59 us
    dot_general x1, matrix products, body(): jnp.dot(piece, q_weight, preferred_element_type=jnp.float32)  8.8 us
    dot_general x1, matrix products, body(): terms = jnp.dot(ordered, out_weight, preferred_element_type=jnp.float32)  8.75 us
    ppermute x4, starting transfers between devices, gather_wide(): other = lax.ppermute(held, WIDE, [(i, i ^ step) for i in range(count)])  7.53 us
    all_to_all x1, waiting for transfers between devices, body(): lax.all_to_all(partial_terms, EVERY, split_axis=0, concat_axis=0, tiled=T...  6.89 us
    all_to_all x1, starting transfers between devices, body(): lax.all_to_all(partial_terms, EVERY, split_axis=0, concat_axis=0, tiled=T...  6.07 us
    all_to_all x1, starting transfers between devices, body(): lax.all_to_all(parts.reshape(high * narrow * per_owner, depth), ('hi', 'n...  3.71 us
  transfers between devices with their start and end apart: 7, of which 7 were waited for; matrix products, arithmetic and copies ran while one was open for 2% of the time, Pallas kernels for 0%

profile of v1, /device:TPU:0, one launch (start us, length us, event | category | flops | bytes accessed | tf_op | source)
XLA Modules:
  0.0 84.6 jit_solution(2509425022528941664)
XLA Ops:
  0.0 4.1 %collective-permute-start = (bf16[2,8192]{1,0:T(2,128)(2,1)}, bf16[2,8192]{1,0:T(2,128)(2,1)S(1)}, u32[]{:S(2)}, u32[]{:S(2)}) collective-permute-start(bf16[2,8192]{1,0:T(2,128)(2,1)} %param.8), channel_id=1, source_target_pairs={{0,16},{2,18},{4,20},{6,22},{8,24},{10,26},{12,28},{14,30},{16,0},... | collective-permute-start | bytes 98312 | tf_op jit(solution)/shard_map/ppermute | solution.py:99
  4.1 2.5 %collective-permute-done = bf16[2,8192]{1,0:T(2,128)(2,1)S(1)} collective-permute-done((bf16[2,8192]{1,0:T(2,128)(2,1)}, bf16[2,8192]{1,0:T(2,128)(2,1)S(1)}, u32[]{:S(2)}, u32[]{:S(2)}) %collective-permute-start) | collective-permute-done | bytes 32800 | tf_op jit(solution)/shard_map/ppermute | solution.py:99
  6.5 0.8 fusion.22
  7.3 0.1 pad_maximum_fusion.3
  7.4 1.6 %collective-permute-start.1 = (bf16[2,2,8192]{2,1,0:T(2,128)(2,1)S(1)}, bf16[2,2,8192]{2,1,0:T(2,128)(2,1)S(1)}, u32[]{:S(2)}, u32[]{:S(2)}) collective-permute-start(bf16[2,2,8192]{2,1,0:T(2,128)(2,1)S(1)} %pad_maximum_fusion.3), channel_id=1, source_target_pairs={{0,8},{2,10},{4,12},{6,14},{8,0},{10,2},{12,4},{14,6},{16,24},{18,... | collective-permute-start | bytes 196616 | tf_op jit(solution)/shard_map/ppermute | solution.py:99
  9.1 2.7 %collective-permute-done.1 = bf16[2,2,8192]{2,1,0:T(2,128)(2,1)S(1)} collective-permute-done((bf16[2,2,8192]{2,1,0:T(2,128)(2,1)S(1)}, bf16[2,2,8192]{2,1,0:T(2,128)(2,1)S(1)}, u32[]{:S(2)}, u32[]{:S(2)}) %collective-permute-start.1) | collective-permute-done | bytes 65568 | tf_op jit(solution)/shard_map/ppermute | solution.py:99
  11.8 0.2 fusion.13
  11.9 0.2 pad_maximum_fusion.2
  12.1 1.8 %collective-permute-start.2 = (bf16[2,2,2,8192]{3,2,0,1:T(2,128)(2,1)S(1)}, bf16[2,2,2,8192]{3,2,0,1:T(2,128)(2,1)S(1)}, u32[]{:S(2)}, u32[]{:S(2)}) collective-permute-start(bf16[2,2,2,8192]{3,2,0,1:T(2,128)(2,1)S(1)} %pad_maximum_fusion.2), channel_id=1, source_target_pairs={{0,4},{2,6},{4,0},{6,2},{8,12},{10,14},{12,8},{14,10},{16,20},{18,... | collective-permute-start | bytes 393224 | tf_op jit(solution)/shard_map/ppermute | solution.py:99
  13.9 3.3 %collective-permute-done.2 = bf16[2,2,2,8192]{3,2,0,1:T(2,128)(2,1)S(1)} collective-permute-done((bf16[2,2,2,8192]{3,2,0,1:T(2,128)(2,1)S(1)}, bf16[2,2,2,8192]{3,2,0,1:T(2,128)(2,1)S(1)}, u32[]{:S(2)}, u32[]{:S(2)}) %collective-permute-start.2) | collective-permute-done | bytes 131104 | tf_op jit(solution)/shard_map/ppermute | solution.py:99
  17.2 0.3 fusion.8
  17.5 0.4 pad_maximum_fusion.1
  17.9 1.5 %collective-permute-done.3 = bf16[2,2,2,2,8192]{4,3,0,1,2:T(2,128)(2,1)S(1)} collective-permute-done((bf16[2,2,2,2,8192]{4,3,0,1,2:T(2,128)(2,1)S(1)}, bf16[2,2,2,2,8192]{4,3,0,1,2:T(2,128)(2,1)S(1)}, u32[]{:S(2)}, u32[]{:S(2)}) %collective-permute-start.3) | collective-permute-done | bytes 262176 | tf_op jit(solution)/shard_map/ppermute | solution.py:99
  19.4 0.6 fusion.6
  20.1 0.7 pad_maximum_fusion
  20.8 0.4 copy.25
  21.2 0.2 reshape.284
  21.4 8.8 %fusion.36 = f32[32,1024]{1,0:T(8,128)S(1)} fusion(bf16[32,8192]{1,0:T(8,128)(2,1)S(1)} %reshape.284, bf16[8192,1024]{1,0:T(8,128)(2,1)} %param.9), kind=kOutput, calls=%fused_computation.70 | convolution fusion | flops 536870912 | bytes 17432576 | tf_op jit(solution)/shard_map/dot_general | solution.py:129
  30.2 0.4 fusion.37
  30.7 0.8 copy.26
  31.5 6.1 %all-to-all-start = ((f32[32,1,1152]{2,1,0:T(1,128)}), f32[32,1,1152]{2,1,0:T(1,128)S(1)}, u32[]{:S(2)}, u32[]{:S(2)}) async-start(f32[32,1,1152]{2,1,0:T(1,128)} %copy.26), calls=%async_computation | async-start | bytes 294912 | tf_op jit(solution)/shard_map/all_to_all | solution.py:134
  38.3 0.1 copy.34
  38.4 1.1 %copy.36 = bf16[32,8,8,128]{3,2,1,0:T(8,128)(2,1)S(1)} copy(bf16[32,8,8,128]{3,1,2,0:T(8,128)(2,1)} %bitcast.62) | data formatting | bytes 1048576
  39.6 6.9 %all-to-all-done = f32[32,1,1152]{2,1,0:T(1,128)S(1)} async-done(((f32[32,1,1152]{2,1,0:T(1,128)}), f32[32,1,1152]{2,1,0:T(1,128)S(1)}, u32[]{:S(2)}, u32[]{:S(2)}) %all-to-all-start) | async-done | bytes 147488 | tf_op jit(solution)/shard_map/all_to_all | solution.py:134
  46.5 0.3 reduce.6
  46.9 0.2 reduce_sum.27
  47.4 0.2 multiply_reduce_fusion
  47.6 0.4 fusion.35
  48.0 0.2 fusion.10
  48.2 0.2 fusion.3
  48.5 0.1 broadcast_in_dim.40
  48.6 0.3 all_to_all.16
  48.9 0.5 broadcast.107
  49.4 2.2 %reduce.8 = bf16[16,8192]{1,0:T(8,128)(2,1)S(1)} reduce(bf16[16,1,8192]{2,1,0:T(2,128)(2,1)S(1)} %all_to_all.16, bf16[]{:T(256)} %broadcast.107), dimensions={1}, to_apply=%all_to_all.16.reduce_sub_computation | reduce | bytes 524290 | tf_op jit(solution)/shard_map/all_to_all | solution.py:147
  51.6 0.9 %reshape.300 = bf16[16,2,4096]{2,1,0:T(2,128)(2,1)} reshape(bf16[16,8192]{1,0:T(8,128)(2,1)S(1)} %reduce.8) | data formatting | bytes 524288
  52.5 3.7 %all-to-all-start.1 = ((bf16[16,2,4096]{2,1,0:T(2,128)(2,1)}), bf16[16,2,4096]{2,1,0:T(2,128)(2,1)S(1)}, u32[]{:S(2)}, u32[]{:S(2)}) async-start(bf16[16,2,4096]{2,1,0:T(2,128)(2,1)} %reshape.300), calls=%async_computation.1 | async-start | bytes 524288 | tf_op jit(solution)/shard_map/all_to_all | solution.py:147
  56.2 9.6 %all-to-all-done.1 = bf16[16,2,4096]{2,1,0:T(2,128)(2,1)S(1)} async-done(((bf16[16,2,4096]{2,1,0:T(2,128)(2,1)}), bf16[16,2,4096]{2,1,0:T(2,128)(2,1)S(1)}, u32[]{:S(2)}, u32[]{:S(2)}) %all-to-all-start.1) | async-done | bytes 262176 | tf_op jit(solution)/shard_map/all_to_all | solution.py:147
  65.8 0.3 reshape.301
  66.1 1.5 %reduce.7 = bf16[16,8192]{1,0:T(8,128)(2,1)S(1)} reduce(bf16[16,1,8192]{2,1,0:T(2,128)(2,1)S(1)} %reshape.301, bf16[]{:T(256)} %constant.46), dimensions={1}, to_apply=%all_to_all.15.reduce_sub_computation | reduce | bytes 524290 | tf_op jit(solution)/shard_map/all_to_all | solution.py:147
  67.6 0.2 reshape.291
  67.8 0.2 copy.30
  67.9 2.2 %all_gather.3 = bf16[8,2,2,8192]{3,0,2,1:T(8,128)(2,1)S(1)} all-gather(bf16[8,1,2,8192]{3,0,2,1:T(8,128)(2,1)S(1)} %copy.30), channel_id=1, replica_groups=mesh['hi'=8,'lo'=2,'narrow'=2] {'lo'}, dimensions={1}, use_global_device_ids=true | all-gather | bytes 786432 | tf_op jit(solution)/shard_map/all_gather | solution.py:154
  70.1 0.5 copy.31
  70.7 0.2 dot_general.21
  70.9 8.7 %fusion = f32[2,16,1024]{2,1,0:T(8,128)S(1)} fusion(bf16[2,16,8192]{2,1,0:T(8,128)(2,1)S(1)} %dot_general.21, bf16[8192,1024]{1,0:T(8,128)(2,1)} %param.11), kind=kOutput, calls=%fused_computation | convolution fusion | flops 536870912 | bytes 17432576 | tf_op jit(solution)/shard_map/dot_general | solution.py:156
  79.6 0.9 %collective-permute-start.4 = (f32[16,1024]{1,0:T(8,128)S(1)}, f32[16,1024]{1,0:T(8,128)S(1)}, u32[]{:S(2)}, u32[]{:S(2)}) collective-permute-start(f32[16,1024]{1,0:T(8,128)S(1)} %dynamic-slice_bitcast_fusion), channel_id=1, source_target_pairs={{0,1},{1,0},{2,3},{3,2},{4,5},{5,4},{6,7},{7,6},{8,9},{9,8},{10,11... | collective-permute-start | bytes 196616 | tf_op jit(solution)/shard_map/ppermute | solution.py:169
  80.5 3.5 %collective-permute-done.4 = f32[16,1024]{1,0:T(8,128)S(1)} collective-permute-done((f32[16,1024]{1,0:T(8,128)S(1)}, f32[16,1024]{1,0:T(8,128)S(1)}, u32[]{:S(2)}, u32[]{:S(2)}) %collective-permute-start.4) | collective-permute-done | bytes 65568 | tf_op jit(solution)/shard_map/ppermute | solution.py:169
  84.0 0.6 fusion.18
  (23 shorter events, 0.6 us)
Async XLA Ops:
  0.0 30.2 %copy-start = (bf16[8192,128]{1,0:T(8,128)(2,1)S(1)}, bf16[8192,128]{1,0:T(8,128)(2,1)}, u32[]{:S(2)}) copy-start(bf16[8192,128]{1,0:T(8,128)(2,1)} %param.10) | copy-start | bytes 6291460
  0.0 6.5 %collective-permute-start = (bf16[2,8192]{1,0:T(2,128)(2,1)}, bf16[2,8192]{1,0:T(2,128)(2,1)S(1)}, u32[]{:S(2)}, u32[]{:S(2)}) collective-permute-start(bf16[2,8192]{1,0:T(2,128)(2,1)} %param.8), channel_id=1, source_target_pairs={{0,16},{2,18},{4,20},{6,22},{8,24},{10,26},{12,28},{14,30},{16,0},... | collective-permute-start | bytes 98312 | tf_op jit(solution)/shard_map/ppermute | solution.py:99
  7.4 4.3 %collective-permute-start.1 = (bf16[2,2,8192]{2,1,0:T(2,128)(2,1)S(1)}, bf16[2,2,8192]{2,1,0:T(2,128)(2,1)S(1)}, u32[]{:S(2)}, u32[]{:S(2)}) collective-permute-start(bf16[2,2,8192]{2,1,0:T(2,128)(2,1)S(1)} %pad_maximum_fusion.3), channel_id=1, source_target_pairs={{0,8},{2,10},{4,12},{6,14},{8,0},{10,2},{12,4},{14,6},{16,24},{18,... | collective-permute-start | bytes 196616 | tf_op jit(solution)/shard_map/ppermute | solution.py:99
  12.1 5.0 %collective-permute-start.2 = (bf16[2,2,2,8192]{3,2,0,1:T(2,128)(2,1)S(1)}, bf16[2,2,2,8192]{3,2,0,1:T(2,128)(2,1)S(1)}, u32[]{:S(2)}, u32[]{:S(2)}) collective-permute-start(bf16[2,2,2,8192]{3,2,0,1:T(2,128)(2,1)S(1)} %pad_maximum_fusion.2), channel_id=1, source_target_pairs={{0,4},{2,6},{4,0},{6,2},{8,12},{10,14},{12,8},{14,10},{16,20},{18,... | collective-permute-start | bytes 393224 | tf_op jit(solution)/shard_map/ppermute | solution.py:99
  17.8 1.6 %collective-permute-start.3 = (bf16[2,2,2,2,8192]{4,3,0,1,2:T(2,128)(2,1)S(1)}, bf16[2,2,2,2,8192]{4,3,0,1,2:T(2,128)(2,1)S(1)}, u32[]{:S(2)}, u32[]{:S(2)}) collective-permute-start(bf16[2,2,2,2,8192]{4,3,0,1,2:T(2,128)(2,1)S(1)} %pad_maximum_fusion.1), channel_id=1, source_target_pairs={{0,2},{2,0},{4,6},{6,4},{8,10},{10,8},{12,14},{14,12},{16,18},{18,... | collective-permute-start | bytes 786440 | tf_op jit(solution)/shard_map/ppermute | solution.py:99
  21.2 26.4 %copy-start.2 = (f32[1,1024]{1,0:T(1,128)S(1)}, f32[1,1024]{1,0:T(1,128)}, u32[]{:S(2)}) copy-start(f32[1,1024]{1,0:T(1,128)} %param.14) | copy-start | bytes 12292
  21.4 16.8 %copy-start.1 = (bf16[1,256,1024]{2,1,0:T(8,128)(2,1)S(1)}, bf16[1,256,1024]{2,1,0:T(8,128)(2,1)}, u32[]{:S(2)}) copy-start(bf16[1,256,1024]{2,1,0:T(8,128)(2,1)} %param.12) | copy-start | bytes 1572868
  31.5 14.9 %all-to-all-start = ((f32[32,1,1152]{2,1,0:T(1,128)}), f32[32,1,1152]{2,1,0:T(1,128)S(1)}, u32[]{:S(2)}, u32[]{:S(2)}) async-start(f32[32,1,1152]{2,1,0:T(1,128)} %copy.26), calls=%async_computation | async-start | bytes 294912 | tf_op jit(solution)/shard_map/all_to_all | solution.py:134
  52.5 13.3 %all-to-all-start.1 = ((bf16[16,2,4096]{2,1,0:T(2,128)(2,1)}), bf16[16,2,4096]{2,1,0:T(2,128)(2,1)S(1)}, u32[]{:S(2)}, u32[]{:S(2)}) async-start(bf16[16,2,4096]{2,1,0:T(2,128)(2,1)} %reshape.300), calls=%async_computation.1 | async-start | bytes 524288 | tf_op jit(solution)/shard_map/all_to_all | solution.py:147
  79.6 4.3 %collective-permute-start.4 = (f32[16,1024]{1,0:T(8,128)S(1)}, f32[16,1024]{1,0:T(8,128)S(1)}, u32[]{:S(2)}, u32[]{:S(2)}) collective-permute-start(f32[16,1024]{1,0:T(8,128)S(1)} %dynamic-slice_bitcast_fusion), channel_id=1, source_target_pairs={{0,1},{1,0},{2,3},{3,2},{4,5},{5,4},{6,7},{7,6},{8,9},{9,8},{10,11... | collective-permute-start | bytes 196616 | tf_op jit(solution)/shard_map/ppermute | solution.py:169

commit v2 on v1

--- a/solution.py
+++ b/solution.py
@@ -1,8 +1,11 @@
+import functools
 import math
 
 import jax
 import jax.numpy as jnp
 from jax import lax
+from jax.experimental import pallas as pl
+from jax.experimental.pallas import tpu as pltpu
 from jax.sharding import Mesh
 from jax.sharding import PartitionSpec as P
 
@@ -106,7 +109,7 @@
     return held.reshape((count * block.shape[0],) + block.shape[1:])
 
 
-def body(
+def general_body(
     tokens,
     q_weight,
     key_value_weight,
@@ -172,6 +175,361 @@
     return total
 
 
+WHOLE = pl.BlockSpec(memory_space=pltpu.VMEM)
+LANES = 128
+
+
+def params(mebibytes):
+    return pltpu.CompilerParams(vmem_limit_bytes=mebibytes << 20)
+
+
+def join_kernel(a_ref, b_ref, _, o_ref):
+    rows = a_ref.shape[0]
+    o_ref[:rows] = a_ref[...]
+    o_ref[rows:] = b_ref[...]
+
+
+def join(a, b, ready):
+    ready = pltpu.with_memory_space_constraint(ready, pltpu.VMEM)
+    return pl.pallas_call(
+        join_kernel,
+        out_shape=jax.ShapeDtypeStruct((2 * a.shape[0],) + a.shape[1:], a.dtype),
+        in_specs=[WHOLE] * 3,
+        out_specs=WHOLE,
+        compiler_params=params(2),
+        cost_estimate=pl.CostEstimate(flops=0, bytes_accessed=8 * a.size, transcendentals=0),
+        name="join_rows",
+    )(a, b, ready)
+
+
+def place_rows(piece_ref, turned, block, first, blocks):
+    tiles = piece_ref.shape[1]
+    for j in range(piece_ref.shape[0] // block):
+        at = pl.multiple_of(blocks(j) * (block * tiles), block * tiles)
+        turned[pl.ds(at, block * tiles), :] = (
+            piece_ref[j * block : (j + 1) * block].reshape(block * tiles, LANES).astype(jnp.float32)
+        )
+
+
+def turned_rows(turned, rows, tiles, first, count):
+    return jnp.concatenate(
+        [turned[pl.ds(first + t, rows, stride=tiles), :] for t in range(count)], axis=1
+    ).astype(jnp.bfloat16)
+
+
+def opening_kernel(tokens_ref, length_ref, rows_ref, turn_ref, length_row_ref):
+    rows, tiles, _ = rows_ref.shape
+    values = tokens_ref[...].astype(jnp.float32)
+    for r in range(rows):
+        rows_ref[r] = jnp.concatenate(
+            [values[r : r + 1, t * LANES : (t + 1) * LANES] for t in range(tiles)], axis=0
+        ).astype(jnp.bfloat16)
+    half = HEAD_SIZE // 2
+    lane = lax.broadcasted_iota(jnp.int32, (1, HEAD_SIZE), 1)
+    index = jnp.where(lane < half, lane, lane - half).astype(jnp.float32)
+    freq = jnp.exp(index * (-2.0 * math.log(500000.0) / HEAD_SIZE))
+    length = jnp.broadcast_to(length_ref[...], (1, HEAD_SIZE))
+    angle = length.astype(jnp.float32) * freq
+    sine = jnp.sin(angle)
+    turn_ref[0:1] = jnp.cos(angle)
+    turn_ref[1:2] = jnp.where(lane < half, -sine, sine)
+    length_row_ref[...] = length
+
+
+def opening(tokens, lengths):
+    rows, width = tokens.shape
+    return pl.pallas_call(
+        opening_kernel,
+        out_shape=(
+            jax.ShapeDtypeStruct((rows, width // LANES, LANES), tokens.dtype),
+            jax.ShapeDtypeStruct((2, HEAD_SIZE), jnp.float32),
+            jax.ShapeDtypeStruct((1, HEAD_SIZE), jnp.int32),
+        ),
+        in_specs=[WHOLE] * 2,
+        out_specs=(WHOLE,) * 3,
+        compiler_params=params(2),
+        cost_estimate=pl.CostEstimate(flops=0, bytes_accessed=4 * tokens.size, transcendentals=0),
+        name="opening",
+    )(tokens, lengths)
+
+
+def load_kernel(first, weight_ref, after_ref, o_ref, sem):
+    rows = o_ref.shape[0]
+    copy = pltpu.make_async_copy(weight_ref.at[pl.ds(first, rows)], o_ref, sem)
+    copy.start()
+    copy.wait()
+
+
+def load(weight, first, rows, after):
+    weight = pltpu.with_memory_space_constraint(weight, pltpu.HBM)
+    return pl.pallas_call(
+        functools.partial(load_kernel, first),
+        out_shape=pltpu.VMEM((rows, weight.shape[1]), weight.dtype),
+        in_specs=[pl.BlockSpec(memory_space=pltpu.HBM), pl.BlockSpec(memory_space=pl.ANY)],
+        out_specs=WHOLE,
+        scratch_shapes=[pltpu.SemaphoreType.DMA],
+        compiler_params=params(1),
+        cost_estimate=pl.CostEstimate(
+            flops=0, bytes_accessed=2 * rows * weight.shape[1], transcendentals=0
+        ),
+        name="load",
+    )(weight, after)
+
+
+def first_product_kernel(own_ref, other_ref, *refs):
+    *q_refs, kv_ref, o_ref, turned = refs
+    me = lax.axis_index(WIDE)
+    pair = 2
+    rows = 2 * own_ref.shape[0]
+    tiles = own_ref.shape[1]
+    count = rows // pair
+    bits = count.bit_length() - 1
+
+    def source(j, last):
+        mask = last
+        for bit in range(bits - 1):
+            if j >> bit & 1:
+                mask |= count >> (bit + 1)
+        return me ^ mask
+
+    place_rows(own_ref, turned, pair, 0, lambda j: source(j, 0))
+    place_rows(other_ref, turned, pair, 0, lambda j: source(j, 1))
+    group = 8
+    deep = group * LANES
+    q_cols, kv_cols = q_refs[0].shape[1], kv_ref.shape[1]
+    totals = jnp.zeros((rows, q_cols), jnp.float32), jnp.zeros((rows, kv_cols), jnp.float32)
+    base = 0
+    for q_ref in q_refs:
+
+        def step(k, carry):
+            q_total, kv_total = carry
+            x = turned_rows(turned, rows, tiles, (base // LANES) + k * group, group)
+            at = pl.multiple_of(k * deep, deep)
+            q_total = q_total + jnp.dot(
+                x, q_ref[pl.ds(at, deep), :], preferred_element_type=jnp.float32
+            )
+            kv_total = kv_total + jnp.dot(
+                x, kv_ref[pl.ds(base + at, deep), :], preferred_element_type=jnp.float32
+            )
+            return q_total, kv_total
+
+        totals = lax.fori_loop(0, q_ref.shape[0] // deep, step, totals)
+        base += q_ref.shape[0]
+    q_total, kv_total = totals
+    for r in range(rows):
+        o_ref[r, :, :q_cols] = q_total[r : r + 1]
+        o_ref[r, :, q_cols:] = kv_total[r : r + 1]
+
+
+def first_product(own, other, q_parts, kv_weight):
+    rows = 2 * own.shape[0]
+    depth = kv_weight.shape[0]
+    width = q_parts[0].shape[1] + kv_weight.shape[1]
+    weights = [pltpu.with_memory_space_constraint(w, pltpu.VMEM) for w in (*q_parts, kv_weight)]
+    return pl.pallas_call(
+        first_product_kernel,
+        out_shape=jax.ShapeDtypeStruct((rows, 1, width), jnp.float32),
+        in_specs=[WHOLE] * (2 + len(weights)),
+        out_specs=WHOLE,
+        scratch_shapes=[pltpu.VMEM((rows * own.shape[1], LANES), jnp.float32)],
+        compiler_params=params(6),
+        cost_estimate=pl.CostEstimate(
+            flops=2 * rows * depth * width,
+            bytes_accessed=4 * own.size + 2 * depth * width,
+            transcendentals=0,
+        ),
+        name="first_product",
+    )(own, other, *weights)
+
+
+def second_product_kernel(own_ref, other_ref, w_ref, keep_ref, send_ref, turned, w_buf, sems):
+    low = lax.axis_index("lo")
+    mine = lax.axis_index("narrow")
+    chunks = w_buf.shape[0]
+    deep = w_buf.shape[1]
+    copies = [
+        pltpu.make_async_copy(w_ref.at[pl.ds(c * deep, deep)], w_buf.at[c], sems.at[c])
+        for c in range(chunks)
+    ]
+    for copy in copies:
+        copy.start()
+    pair = 2
+    rows = 2 * own_ref.shape[0]
+    tiles = own_ref.shape[1]
+    place_rows(own_ref, turned, pair, 0, lambda j: 2 * j + low)
+    place_rows(other_ref, turned, pair, 0, lambda j: 2 * j + (1 - low))
+    group = deep // LANES
+    total = jnp.zeros((rows, w_ref.shape[1]), jnp.float32)
+    for c in range(chunks):
+        x = turned_rows(turned, rows, tiles, c * group, group)
+        copies[c].wait()
+        total = total + jnp.dot(x, w_buf[c], preferred_element_type=jnp.float32)
+    half = rows // 2
+    lower = mine == 0
+    keep_ref[...] = jnp.where(lower, total[:half], total[half:])
+    send_ref[...] = jnp.where(lower, total[half:], total[:half])
+
+
+def second_product(own, other, weight):
+    rows = 2 * own.shape[0]
+    cols = weight.shape[1]
+    chunks = 8
+    weight = pltpu.with_memory_space_constraint(weight, pltpu.HBM)
+    half = jax.ShapeDtypeStruct((rows // 2, cols), jnp.float32)
+    return pl.pallas_call(
+        second_product_kernel,
+        out_shape=(half, half),
+        in_specs=[WHOLE, WHOLE, pl.BlockSpec(memory_space=pltpu.HBM)],
+        out_specs=(WHOLE, WHOLE),
+        scratch_shapes=[
+            pltpu.VMEM((rows * own.shape[1], LANES), jnp.float32),
+            pltpu.VMEM((chunks, weight.shape[0] // chunks, cols), weight.dtype),
+            pltpu.SemaphoreType.DMA((chunks,)),
+        ],
+        compiler_params=params(24),
+        cost_estimate=pl.CostEstimate(
+            flops=2 * rows * weight.size, bytes_accessed=4 * own.size + 2 * weight.size, transcendentals=0
+        ),
+        name="second_product",
+    )(own, other, weight)
+
+
+def attention_kernel(length_ref, got_ref, keys_ref, values_ref, scale_ref, turn_ref, o_ref):
+    copies, parts, per_part, _ = o_ref.shape
+    heads_of = (got_ref.shape[2] - LANES) // LANES
+    group = QUERY_HEADS // KEY_VALUE_HEADS
+    sources = group // heads_of
+    q_cols = heads_of * LANES
+    slots = keys_ref.shape[1]
+    inverse_scale = HEAD_SIZE ** (-0.5)
+    cosine, sine = turn_ref[0:1], turn_ref[1:2]
+
+    def rounded(w, at, size):
+        total = got_ref[2 * w, :, at : at + size] + got_ref[2 * w + 1, :, at : at + size]
+        return total.astype(jnp.bfloat16).astype(jnp.float32)
+
+    def rotate(x):
+        return x * cosine + pltpu.roll(x, HEAD_SIZE // 2, 1) * sine
+
+    live = lax.broadcasted_iota(jnp.int32, (group, slots), 1) < jnp.concatenate(
+        [length_ref[...]] * (slots // LANES), axis=1
+    )
+    for g in range(KEY_VALUE_HEADS):
+        span = slice(g * HEAD_SIZE, (g + 1) * HEAD_SIZE)
+        rows = []
+        for w in range(g * sources, (g + 1) * sources):
+            row = rounded(w, 0, q_cols)
+            rows += [row[:, i * LANES : (i + 1) * LANES] for i in range(heads_of)]
+        rotated = rotate(jnp.concatenate(rows, axis=0))
+        fresh_key = rotate(rounded(g, q_cols, LANES)).astype(jnp.bfloat16).astype(jnp.float32)
+        fresh_value = rounded(KEY_VALUE_HEADS + g, q_cols, LANES)
+        cache_query = (rotated * scale_ref[:, span] * inverse_scale).astype(jnp.bfloat16)
+        fresh_query = (rotated * inverse_scale).astype(jnp.bfloat16).astype(jnp.float32)
+        scores = lax.dot_general(
+            cache_query,
+            keys_ref[0, :, span],
+            (((1,), (1,)), ((), ())),
+            preferred_element_type=jnp.float32,
+        )
+        fresh_score = jnp.sum(fresh_query * fresh_key, axis=-1, keepdims=True)
+        masked = jnp.where(live, scores, jnp.float32(-1e30))
+        top = jnp.maximum(jnp.max(masked, axis=-1, keepdims=True), fresh_score)
+        exps = jnp.where(live, jnp.exp(masked - top), jnp.float32(0.0))
+        fresh_exp = jnp.exp(fresh_score - top)
+        total = jnp.sum(exps, axis=-1, keepdims=True) + fresh_exp
+        summed = jnp.dot(
+            exps.astype(jnp.bfloat16), values_ref[0, :, span], preferred_element_type=jnp.float32
+        )
+        summed = summed + fresh_exp.astype(jnp.bfloat16).astype(jnp.float32) * fresh_value
+        attended = (summed / total).astype(jnp.bfloat16)
+        part, at = divmod(g * group, per_part)
+        for copy in range(copies):
+            o_ref[copy, part, at : at + group, :] = attended
+
+
+def attention(got, keys, values, scale, lengths, turn, copies, parts):
+    keys = pltpu.with_memory_space_constraint(keys, pltpu.VMEM)
+    values = pltpu.with_memory_space_constraint(values, pltpu.VMEM)
+    return pl.pallas_call(
+        attention_kernel,
+        out_shape=jax.ShapeDtypeStruct((copies, parts, QUERY_HEADS // parts, HEAD_SIZE), jnp.bfloat16),
+        in_specs=[WHOLE] * 6,
+        out_specs=WHOLE,
+        compiler_params=params(8),
+        cost_estimate=pl.CostEstimate(
+            flops=4 * QUERY_HEADS * keys.shape[1] * HEAD_SIZE,
+            bytes_accessed=4 * keys.size,
+            transcendentals=QUERY_HEADS * keys.shape[1],
+        ),
+        name="attention",
+    )(lengths, got, keys, values, scale, turn)
+
+
+def fits(tokens, q_weight, key_value_weight, stored_keys):
+    return (
+        lax.axis_size(WIDE) == 16
+        and lax.axis_size("narrow") == 2
+        and tokens.shape[0] == 2
+        and stored_keys.shape[0] == 1
+        and q_weight.shape[1] % 1024 == 0
+        and key_value_weight.shape[1] == LANES
+        and q_weight.shape[0] % 8192 == 0
+    )
+
+
+def tiled_body(
+    tokens,
+    q_weight,
+    key_value_weight,
+    out_weight,
+    stored_keys,
+    stored_values,
+    channel_key_scale,
+    lengths,
+):
+    count = lax.axis_size(WIDE)
+    narrow = lax.axis_size("narrow")
+    held, turn, lengths = opening(tokens, lengths.reshape(1, 1))
+    eighth = q_weight.shape[0] // 8
+    q_parts = []
+    for step, first, last in ((8, 0, 2), (4, 2, 5), (2, 5, 8)):
+        other = lax.ppermute(held, WIDE, [(i, i ^ step) for i in range(count)])
+        part = load(q_weight, first * eighth, (last - first) * eighth, held)
+        held = join(held, other, part)
+        q_parts.append(part)
+    other = lax.ppermute(held, WIDE, [(i, i ^ 1) for i in range(count)])
+    kv_part = load(key_value_weight, 0, key_value_weight.shape[0], held)
+    partial_terms = first_product(held, other, q_parts, kv_part)
+    got = lax.all_to_all(partial_terms, EVERY, split_axis=0, concat_axis=0, tiled=True)
+    attended = attention(
+        got,
+        stored_keys,
+        stored_values,
+        channel_key_scale,
+        lengths,
+        turn,
+        lax.axis_size("hi"),
+        narrow,
+    )
+    mine = lax.all_to_all(
+        attended.reshape((-1,) + attended.shape[2:]),
+        ("hi", "narrow"),
+        split_axis=0,
+        concat_axis=0,
+        tiled=True,
+    )
+    other = lax.ppermute(mine, "lo", [(0, 1), (1, 0)])
+    keep, send = second_product(mine, other, out_weight)
+    return (keep + lax.ppermute(send, "narrow", [(0, 1), (1, 0)])).astype(jnp.bfloat16)
+
+
+def body(*arguments):
+    tokens, q_weight, key_value_weight, _, stored_keys = arguments[:5]
+    if fits(tokens, q_weight, key_value_weight, stored_keys):
+        return tiled_body(*arguments)
+    return general_body(*arguments)
+
+
 def solution(mesh):
     high, low, narrow = mesh.shape["wide"] // 2, 2, mesh.shape["narrow"]
     fine = Mesh(mesh.devices.reshape(high, low, narrow), EVERY)

time: 85 us -> 66 us (0.78)
  blocking collectives: 2.18 us -> 27.1 us
  waiting for transfers between devices: 29.9 us -> 5.72 us
  Pallas kernels: 0 us -> 22.4 us
  matrix products: 18.6 us -> 0 us
  starting transfers between devices: 18.2 us -> 8.25 us
  other arithmetic: 8.82 us -> 0.62 us
  local copies, waits for them, and re-layouts: 5.92 us -> 0.77 us
    all_to_all x0 -> x2, blocking collectives: none -> 27.1 us  [the longest x1 14.7 us: tiled_body(): lax.all_to_all(partial_terms, EVERY, split_axis=0, concat_axis=0, tiled=T...]
    pallas_call x0 -> x11, Pallas kernels: none -> 22.4 us  [the longest x4 9.38 us: load(): pl.pallas_call(functools.partial(load_kernel, first), out_shape=pltpu.VME...]
    dot_general x5 -> x0, matrix products: 18.6 us -> none  [the longest x1 8.8 us: body(): jnp.dot(piece, q_weight, preferred_element_type=jnp.float32)]
    all_to_all x2 -> x0, waiting for transfers between devices: 16.5 us -> none  [the longest x1 9.59 us: body(): lax.all_to_all(parts.reshape(high * narrow * per_owner, depth), ('hi', 'n...]
    all_to_all x2 -> x0, starting transfers between devices: 9.78 us -> none  [the longest x1 6.07 us: body(): lax.all_to_all(partial_terms, EVERY, split_axis=0, concat_axis=0, tiled=T...]
    ppermute x5 -> x6, waiting for transfers between devices: 13.4 us -> 5.72 us  [the longest x1 3.5 us: tiled_body(): lax.ppermute(send, 'narrow', [(0, 1), (1, 0)])]
    all_to_all x4 -> x0, other arithmetic: 4.05 us -> none  [the longest x2 3.69 us: body(): lax.all_to_all(parts.reshape(high * narrow * per_owner, depth), ('hi', 'n...]
    another operation x8 -> x0, other arithmetic: 3.28 us -> none  [gather_wide(): jnp.stack([jnp.where(upper, other, held), jnp.where(upper, held, other)],...]
  transfers between devices with their start and end apart: 7 -> 6, of which waited for: 7 -> 3; matrix products, arithmetic and copies ran while one was open for 2% -> 0% of each run, Pallas kernels for 0% -> 14%
where the time goes in v2:
time: 66 us; the launch traced here: 65.6 us
  blocking collectives  27.1 us (41%)
  Pallas kernels  22.4 us (34%)
  starting transfers between devices  8.25 us (12%)
  waiting for transfers between devices  5.72 us (9%)
  between operations  0.78 us (1%)
  local copies, waits for them, and re-layouts  0.77 us (1%)
    all_to_all x1, blocking collectives, tiled_body(): lax.all_to_all(partial_terms, EVERY, split_axis=0, concat_axis=0, tiled=T...  14.7 us
    all_to_all x1, blocking collectives, tiled_body(): lax.all_to_all(attended.reshape((-1,) + attended.shape[2:]), ('hi', 'narr...  12.4 us
    pallas_call x4, Pallas kernels, load(): pl.pallas_call(functools.partial(load_kernel, first), out_shape=pltpu.VME...  9.38 us
    ppermute x3, starting transfers between devices, tiled_body(): other = lax.ppermute(held, WIDE, [(i, i ^ step) for i in range(count)])  7.34 us
    pallas_call x1, Pallas kernels, second_product(): pl.pallas_call(second_product_kernel, out_shape=(half, half), in_specs=[W...  6.4 us
    pallas_call x1, Pallas kernels, first_product(): pl.pallas_call(first_product_kernel, out_shape=jax.ShapeDtypeStruct((rows...  4.36 us
    ppermute x1, waiting for transfers between devices, tiled_body(): lax.ppermute(send, 'narrow', [(0, 1), (1, 0)])  3.5 us
    pallas_call x1, Pallas kernels, attention(): pl.pallas_call(attention_kernel, out_shape=jax.ShapeDtypeStruct((copies,...  2.06 us
  transfers between devices with their start and end apart: 6, of which 3 were waited for; matrix products, arithmetic and copies ran while one was open for 0% of the time, Pallas kernels for 14%

profile of v2, /device:TPU:0, one launch (start us, length us, event | category | flops | bytes accessed | tf_op | source)
XLA Modules:
  0.0 65.6 jit_solution(3403944156740952182)
XLA Ops:
  0.7 0.0 copy-start.2
  0.7 0.7 %copy-done.2 = bf16[2,8192]{1,0:T(2,128)(2,1)S(1)} copy-done((bf16[2,8192]{1,0:T(2,128)(2,1)S(1)}, bf16[2,8192]{1,0:T(2,128)(2,1)}, u32[]{:S(2)}) %copy-start.2) | copy-done | bytes 32792
  1.4 0.1 opening.1
  1.5 4.1 %collective-permute-start = (bf16[2,64,128]{2,1,0:T(8,128)(2,1)S(1)}, bf16[2,64,128]{2,1,0:T(8,128)(2,1)S(1)}, u32[]{:S(2)}, u32[]{:S(2)}) collective-permute-start(bf16[2,64,128]{2,1,0:T(8,128)(2,1)S(1)} %get-tuple-element.11.after_ref.a_ref), channel_id=1, source_target_pairs={{0,16},{2,18},{4,20},{6,22},{8,24},{10,26},{12,28},{14,30},{16,0},... | collective-permute-start | bytes 98312 | tf_op jit(solution)/shard_map/ppermute | solution.py:496
  5.7 2.2 %load.4._.refs_0_ = bf16[2048,1024]{1,0:T(8,128)(2,1)S(1)} custom-call(bf16[8192,1024]{1,0:T(8,128)(2,1)} %weight_ref.6, bf16[2,64,128]{2,1,0:T(8,128)(2,1)S(1)} %get-tuple-element.11.after_ref.a_ref), custom_call_target="tpu_custom_call" | custom-call | bytes 4194304 | tf_op jit(solution)/shard_map/load/pallas_call | solution.py:265
  7.9 0.0 collective-permute-done.b_ref
  7.9 1.6 %collective-permute-start.1 = (bf16[4,64,128]{2,1,0:T(8,128)(2,1)S(1)}, bf16[4,64,128]{2,1,0:T(8,128)(2,1)S(1)}, u32[]{:S(2)}, u32[]{:S(2)}) collective-permute-start(bf16[4,64,128]{2,1,0:T(8,128)(2,1)S(1)} %join_rows.3.after_ref.a_ref), channel_id=1, source_target_pairs={{0,8},{2,10},{4,12},{6,14},{8,0},{10,2},{12,4},{14,6},{16,24},{18,... | collective-permute-start | bytes 196616 | tf_op jit(solution)/shard_map/ppermute | solution.py:496
  9.5 2.8 %load.5._.refs_1_ = bf16[3072,1024]{1,0:T(8,128)(2,1)S(1)} custom-call(bf16[8192,1024]{1,0:T(8,128)(2,1)} %weight_ref.6, bf16[4,64,128]{2,1,0:T(8,128)(2,1)S(1)} %join_rows.3.after_ref.a_ref), custom_call_target="tpu_custom_call" | custom-call | bytes 6291456 | tf_op jit(solution)/shard_map/load/pallas_call | solution.py:265
  12.3 0.0 collective-permute-done.1.b_ref
  12.4 1.6 %collective-permute-start.2 = (bf16[8,64,128]{2,1,0:T(8,128)(2,1)S(1)}, bf16[8,64,128]{2,1,0:T(8,128)(2,1)S(1)}, u32[]{:S(2)}, u32[]{:S(2)}) collective-permute-start(bf16[8,64,128]{2,1,0:T(8,128)(2,1)S(1)} %join_rows.4.after_ref.a_ref), channel_id=1, source_target_pairs={{0,4},{2,6},{4,0},{6,2},{8,12},{10,14},{12,8},{14,10},{16,20},{18,... | collective-permute-start | bytes 393224 | tf_op jit(solution)/shard_map/ppermute | solution.py:496
  14.0 2.8 %load.6._.refs_2_ = bf16[3072,1024]{1,0:T(8,128)(2,1)S(1)} custom-call(bf16[8192,1024]{1,0:T(8,128)(2,1)} %weight_ref.6, bf16[8,64,128]{2,1,0:T(8,128)(2,1)S(1)} %join_rows.4.after_ref.a_ref), custom_call_target="tpu_custom_call" | custom-call | bytes 6291456 | tf_op jit(solution)/shard_map/load/pallas_call | solution.py:265
  16.8 0.6 collective-permute-done.2.b_ref
  17.4 0.1 collective-permute-start.3
  17.5 1.6 %load.7.refs_3_ = bf16[8192,128]{1,0:T(8,128)(2,1)S(1)} custom-call(bf16[8192,128]{1,0:T(8,128)(2,1)} %weight_ref.7, bf16[16,64,128]{2,1,0:T(8,128)(2,1)S(1)} %join_rows.5.after_ref.own_ref), custom_call_target="tpu_custom_call" | custom-call | bytes 2097152 | tf_op jit(solution)/shard_map/load/pallas_call | solution.py:265
  19.1 0.0 copy-start
  19.1 0.0 copy-start.1
  19.1 0.0 copy-start.3
  19.1 0.0 collective-permute-done.3.other_ref
  19.2 4.4 %first_product.1 = f32[32,1,1152]{2,1,0:T(1,128)S(1)} custom-call(bf16[16,64,128]{2,1,0:T(8,128)(2,1)S(1)} %join_rows.5.after_ref.own_ref, bf16[16,64,128]{2,1,0:T(8,128)(2,1)S(1)} %collective-permute-done.3.other_ref, bf16[2048,1024]{1,0:T(8,128)(2,1)S(1)} %load.4._.refs_0_, bf16[3072,1024]{1,0:T(8,128)(2,1)S(1)} %load.5._.refs_1_, ...), custom_call_target="tpu_custom_call" | custom-call | flops 603979776 | bytes 19398656 | tf_op jit(solution)/shard_map/first_product/pallas_call | solution.py:329
  23.5 14.7 %all_to_all.10.got_ref = f32[32,1,1152]{2,1,0:T(1,128)S(1)} all-to-all(f32[32,1,1152]{2,1,0:T(1,128)S(1)} %first_product.1), channel_id=1, replica_groups=mesh['hi'=8,'lo'=2,'narrow'=2] {'hi','lo','narrow'}, dimensions={0} | all-to-all | bytes 294912 | tf_op jit(solution)/shard_map/all_to_all | solution.py:503
  38.2 0.0 copy-done
  38.2 0.0 copy-done.1
  38.2 0.0 copy-done.3
  38.2 2.1 %attention.1 = bf16[8,2,64,128]{3,2,1,0:T(8,128)(2,1)S(1)} custom-call(s32[1,128]{1,0:T(1,128)S(1)} %get-tuple-element.10.length_ref, f32[32,1,1152]{2,1,0:T(1,128)S(1)} %all_to_all.10.got_ref, bf16[1,256,1024]{2,1,0:T(8,128)(2,1)S(1)} %copy-done, bf16[1,256,1024]{2,1,0:T(8,128)(2,1)S(1)} %copy-done.1, f32[1,1024]{1,0:T(1,128)S(1)} %copy-done.3, ...), custom_call_target="tpu_custom_call" | custom-call | flops 16777216 | bytes 1048576 | tf_op jit(solution)/shard_map/attention/pallas_call | solution.py:453
  40.3 12.4 %all_to_all.11.own_ref = bf16[16,64,128]{2,1,0:T(8,128)(2,1)S(1)} all-to-all(bf16[16,64,128]{2,1,0:T(8,128)(2,1)S(1)} %bitcast.3), channel_id=1, replica_groups=mesh['hi'=8,'lo'=2,'narrow'=2] {'hi','narrow'}, dimensions={0} | all-to-all | bytes 524288 | tf_op jit(solution)/shard_map/all_to_all | solution.py:514
  52.7 0.0 collective-permute-start.4
  52.7 1.5 %collective-permute-done.4.other_ref = bf16[16,64,128]{2,1,0:T(8,128)(2,1)S(1)} collective-permute-done((bf16[16,64,128]{2,1,0:T(8,128)(2,1)S(1)}, bf16[16,64,128]{2,1,0:T(8,128)(2,1)S(1)}, u32[]{:S(2)}, u32[]{:S(2)}) %collective-permute-start.4) | collective-permute-done | bytes 262176 | tf_op jit(solution)/shard_map/ppermute | solution.py:521
  54.2 6.4 %second_product.1 = (f32[16,1024]{1,0:T(8,128)S(1)}, f32[16,1024]{1,0:T(8,128)S(1)}) custom-call(bf16[16,64,128]{2,1,0:T(8,128)(2,1)S(1)} %all_to_all.11.own_ref, bf16[16,64,128]{2,1,0:T(8,128)(2,1)S(1)} %collective-permute-done.4.other_ref, bf16[8192,1024]{1,0:T(8,128)(2,1)} %w_ref.1), custom_call_target="tpu_custom_call" | custom-call | flops 536870912 | bytes 17301504 | tf_op jit(solution)/shard_map/second_product/pallas_call | solution.py:379
  60.6 0.8 %collective-permute-start.5 = (f32[16,1024]{1,0:T(8,128)S(1)}, f32[16,1024]{1,0:T(8,128)S(1)}, u32[]{:S(2)}, u32[]{:S(2)}) collective-permute-start(f32[16,1024]{1,0:T(8,128)S(1)} %get-tuple-element.14), channel_id=1, source_target_pairs={{0,1},{1,0},{2,3},{3,2},{4,5},{5,4},{6,7},{7,6},{8,9},{9,8},{10,11... | collective-permute-start | bytes 196616 | tf_op jit(solution)/shard_map/ppermute | solution.py:523
  61.5 3.5 %collective-permute-done.5 = f32[16,1024]{1,0:T(8,128)S(1)} collective-permute-done((f32[16,1024]{1,0:T(8,128)S(1)}, f32[16,1024]{1,0:T(8,128)S(1)}, u32[]{:S(2)}, u32[]{:S(2)}) %collective-permute-start.5) | collective-permute-done | bytes 65568 | tf_op jit(solution)/shard_map/ppermute | solution.py:523
  65.0 0.6 add_convert_fusion
  (3 shorter events, 0.0 us)
Async XLA Ops:
  0.7 0.8 %copy-start.2 = (bf16[2,8192]{1,0:T(2,128)(2,1)S(1)}, bf16[2,8192]{1,0:T(2,128)(2,1)}, u32[]{:S(2)}) copy-start(bf16[2,8192]{1,0:T(2,128)(2,1)} %tokens_ref.1) | copy-start | bytes 98308
  1.5 6.4 %collective-permute-start = (bf16[2,64,128]{2,1,0:T(8,128)(2,1)S(1)}, bf16[2,64,128]{2,1,0:T(8,128)(2,1)S(1)}, u32[]{:S(2)}, u32[]{:S(2)}) collective-permute-start(bf16[2,64,128]{2,1,0:T(8,128)(2,1)S(1)} %get-tuple-element.11.after_ref.a_ref), channel_id=1, source_target_pairs={{0,16},{2,18},{4,20},{6,22},{8,24},{10,26},{12,28},{14,30},{16,0},... | collective-permute-start | bytes 98312 | tf_op jit(solution)/shard_map/ppermute | solution.py:496
  7.9 4.4 %collective-permute-start.1 = (bf16[4,64,128]{2,1,0:T(8,128)(2,1)S(1)}, bf16[4,64,128]{2,1,0:T(8,128)(2,1)S(1)}, u32[]{:S(2)}, u32[]{:S(2)}) collective-permute-start(bf16[4,64,128]{2,1,0:T(8,128)(2,1)S(1)} %join_rows.3.after_ref.a_ref), channel_id=1, source_target_pairs={{0,8},{2,10},{4,12},{6,14},{8,0},{10,2},{12,4},{14,6},{16,24},{18,... | collective-permute-start | bytes 196616 | tf_op jit(solution)/shard_map/ppermute | solution.py:496
  12.4 5.0 %collective-permute-start.2 = (bf16[8,64,128]{2,1,0:T(8,128)(2,1)S(1)}, bf16[8,64,128]{2,1,0:T(8,128)(2,1)S(1)}, u32[]{:S(2)}, u32[]{:S(2)}) collective-permute-start(bf16[8,64,128]{2,1,0:T(8,128)(2,1)S(1)} %join_rows.4.after_ref.a_ref), channel_id=1, source_target_pairs={{0,4},{2,6},{4,0},{6,2},{8,12},{10,14},{12,8},{14,10},{16,20},{18,... | collective-permute-start | bytes 393224 | tf_op jit(solution)/shard_map/ppermute | solution.py:496
  17.4 1.7 %collective-permute-start.3 = (bf16[16,64,128]{2,1,0:T(8,128)(2,1)S(1)}, bf16[16,64,128]{2,1,0:T(8,128)(2,1)S(1)}, u32[]{:S(2)}, u32[]{:S(2)}) collective-permute-start(bf16[16,64,128]{2,1,0:T(8,128)(2,1)S(1)} %join_rows.5.after_ref.own_ref), channel_id=1, source_target_pairs={{0,2},{2,0},{4,6},{6,4},{8,10},{10,8},{12,14},{14,12},{16,18},{18,... | collective-permute-start | bytes 786440 | tf_op jit(solution)/shard_map/ppermute | solution.py:500
  19.1 19.1 %copy-start = (bf16[1,256,1024]{2,1,0:T(8,128)(2,1)S(1)}, bf16[1,256,1024]{2,1,0:T(8,128)(2,1)}, u32[]{:S(2)}) copy-start(bf16[1,256,1024]{2,1,0:T(8,128)(2,1)} %keys_ref.1) | copy-start | bytes 1572868
  19.1 19.1 %copy-start.1 = (bf16[1,256,1024]{2,1,0:T(8,128)(2,1)S(1)}, bf16[1,256,1024]{2,1,0:T(8,128)(2,1)}, u32[]{:S(2)}) copy-start(bf16[1,256,1024]{2,1,0:T(8,128)(2,1)} %values_ref.1) | copy-start | bytes 1572868
  19.1 19.1 %copy-start.3 = (f32[1,1024]{1,0:T(1,128)S(1)}, f32[1,1024]{1,0:T(1,128)}, u32[]{:S(2)}) copy-start(f32[1,1024]{1,0:T(1,128)} %scale_ref.1) | copy-start | bytes 12292
  52.7 1.5 %collective-permute-start.4 = (bf16[16,64,128]{2,1,0:T(8,128)(2,1)S(1)}, bf16[16,64,128]{2,1,0:T(8,128)(2,1)S(1)}, u32[]{:S(2)}, u32[]{:S(2)}) collective-permute-start(bf16[16,64,128]{2,1,0:T(8,128)(2,1)S(1)} %all_to_all.11.own_ref), channel_id=1, source_target_pairs={{0,2},{2,0},{1,3},{3,1},{4,6},{6,4},{5,7},{7,5},{8,10},{10,8},{9,1... | collective-permute-start | bytes 786440 | tf_op jit(solution)/shard_map/ppermute | solution.py:521
  60.6 4.3 %collective-permute-start.5 = (f32[16,1024]{1,0:T(8,128)S(1)}, f32[16,1024]{1,0:T(8,128)S(1)}, u32[]{:S(2)}, u32[]{:S(2)}) collective-permute-start(f32[16,1024]{1,0:T(8,128)S(1)} %get-tuple-element.14), channel_id=1, source_target_pairs={{0,1},{1,0},{2,3},{3,2},{4,5},{5,4},{6,7},{7,6},{8,9},{9,8},{10,11... | collective-permute-start | bytes 196616 | tf_op jit(solution)/shard_map/ppermute | solution.py:523

commit v3 on v2

--- a/solution.py
+++ b/solution.py
@@ -217,18 +217,24 @@
     ).astype(jnp.bfloat16)
 
 
-def opening_kernel(tokens_ref, length_ref, rows_ref, turn_ref, length_row_ref):
-    rows, tiles, _ = rows_ref.shape
-    values = tokens_ref[...].astype(jnp.float32)
-    for r in range(rows):
-        rows_ref[r] = jnp.concatenate(
-            [values[r : r + 1, t * LANES : (t + 1) * LANES] for t in range(tiles)], axis=0
-        ).astype(jnp.bfloat16)
+def as_tiles(row, tiles):
+    return jnp.concatenate(
+        [row[:, t * LANES : (t + 1) * LANES] for t in range(tiles)], axis=0
+    ).astype(jnp.bfloat16)
+
+
+def opening_kernel(own_ref, other_ref, length_ref, _, rows_ref, turn_ref, length_row_ref):
+    _, tiles, _ = rows_ref.shape
+    rows = own_ref.shape[0]
+    for i, ref in enumerate((own_ref, other_ref)):
+        values = ref[...].astype(jnp.float32)
+        for r in range(rows):
+            rows_ref[i * rows + r] = as_tiles(values[r : r + 1], tiles)
     half = HEAD_SIZE // 2
     lane = lax.broadcasted_iota(jnp.int32, (1, HEAD_SIZE), 1)
     index = jnp.where(lane < half, lane, lane - half).astype(jnp.float32)
     freq = jnp.exp(index * (-2.0 * math.log(500000.0) / HEAD_SIZE))
-    length = jnp.broadcast_to(length_ref[...], (1, HEAD_SIZE))
+    length = jnp.full((1, HEAD_SIZE), length_ref[0], jnp.int32)
     angle = length.astype(jnp.float32) * freq
     sine = jnp.sin(angle)
     turn_ref[0:1] = jnp.cos(angle)
@@ -236,36 +242,39 @@
     length_row_ref[...] = length
 
 
-def opening(tokens, lengths):
+def opening(tokens, other, lengths, ready):
     rows, width = tokens.shape
+    ready = pltpu.with_memory_space_constraint(ready, pltpu.VMEM)
     return pl.pallas_call(
         opening_kernel,
         out_shape=(
-            jax.ShapeDtypeStruct((rows, width // LANES, LANES), tokens.dtype),
+            jax.ShapeDtypeStruct((2 * rows, width // LANES, LANES), tokens.dtype),
             jax.ShapeDtypeStruct((2, HEAD_SIZE), jnp.float32),
             jax.ShapeDtypeStruct((1, HEAD_SIZE), jnp.int32),
         ),
-        in_specs=[WHOLE] * 2,
+        in_specs=[WHOLE, WHOLE, pl.BlockSpec(memory_space=pltpu.SMEM), WHOLE],
         out_specs=(WHOLE,) * 3,
         compiler_params=params(2),
-        cost_estimate=pl.CostEstimate(flops=0, bytes_accessed=4 * tokens.size, transcendentals=0),
+        cost_estimate=pl.CostEstimate(flops=0, bytes_accessed=8 * tokens.size, transcendentals=0),
         name="opening",
-    )(tokens, lengths)
-
-
-def load_kernel(first, weight_ref, after_ref, o_ref, sem):
+    )(tokens, other, lengths, ready)
+
+
+def load_kernel(first, weight_ref, *refs):
+    *_, o_ref, sem = refs
     rows = o_ref.shape[0]
     copy = pltpu.make_async_copy(weight_ref.at[pl.ds(first, rows)], o_ref, sem)
     copy.start()
     copy.wait()
 
 
-def load(weight, first, rows, after):
+def load(weight, first, rows, *after):
     weight = pltpu.with_memory_space_constraint(weight, pltpu.HBM)
     return pl.pallas_call(
         functools.partial(load_kernel, first),
         out_shape=pltpu.VMEM((rows, weight.shape[1]), weight.dtype),
-        in_specs=[pl.BlockSpec(memory_space=pltpu.HBM), pl.BlockSpec(memory_space=pl.ANY)],
+        in_specs=[pl.BlockSpec(memory_space=pltpu.HBM)]
+        + [pl.BlockSpec(memory_space=pl.ANY)] * len(after),
         out_specs=WHOLE,
         scratch_shapes=[pltpu.SemaphoreType.DMA],
         compiler_params=params(1),
@@ -273,7 +282,7 @@
             flops=0, bytes_accessed=2 * rows * weight.shape[1], transcendentals=0
         ),
         name="load",
-    )(weight, after)
+    )(weight, *after)
 
 
 def first_product_kernel(own_ref, other_ref, *refs):
@@ -418,8 +427,7 @@
         span = slice(g * HEAD_SIZE, (g + 1) * HEAD_SIZE)
         rows = []
         for w in range(g * sources, (g + 1) * sources):
-            row = rounded(w, 0, q_cols)
-            rows += [row[:, i * LANES : (i + 1) * LANES] for i in range(heads_of)]
+            rows.append(rounded(w, 0, q_cols).reshape(heads_of, LANES))
         rotated = rotate(jnp.concatenate(rows, axis=0))
         fresh_key = rotate(rounded(g, q_cols, LANES)).astype(jnp.bfloat16).astype(jnp.float32)
         fresh_value = rounded(KEY_VALUE_HEADS + g, q_cols, LANES)
@@ -489,14 +497,18 @@
 ):
     count = lax.axis_size(WIDE)
     narrow = lax.axis_size("narrow")
-    held, turn, lengths = opening(tokens, lengths.reshape(1, 1))
     eighth = q_weight.shape[0] // 8
     q_parts = []
+    held, held_rows = tokens, []
     for step, first, last in ((8, 0, 2), (4, 2, 5), (2, 5, 8)):
         other = lax.ppermute(held, WIDE, [(i, i ^ step) for i in range(count)])
-        part = load(q_weight, first * eighth, (last - first) * eighth, held)
-        held = join(held, other, part)
+        part = load(q_weight, first * eighth, (last - first) * eighth, *held_rows)
+        if held_rows:
+            held = join(held, other, part)
+        else:
+            held, turn, lengths = opening(tokens, other, lengths, part)
         q_parts.append(part)
+        held_rows = [held]
     other = lax.ppermute(held, WIDE, [(i, i ^ 1) for i in range(count)])
     kv_part = load(key_value_weight, 0, key_value_weight.shape[0], held)
     partial_terms = first_product(held, other, q_parts, kv_part)

time: 66 us -> 64.7 us (0.980)
  local copies, waits for them, and re-layouts: 0.77 us -> 0.02 us
    unnamed x8, local copies, waits for them, and re-layouts: 0.77 us -> 0.02 us
  transfers between devices with their start and end apart: 6 -> 6, of which waited for: 3 -> 3; matrix products, arithmetic and copies ran while one was open for 0% -> 0% of each run, Pallas kernels for 14% -> 15%
where the time goes in v3:
time: 64.7 us; the launch traced here: 64.4 us
  blocking collectives  26.7 us (41%)
  Pallas kernels  22.4 us (35%)
  starting transfers between devices  8.17 us (13%)
  waiting for transfers between devices  5.72 us (9%)
  between operations  0.8 us (1%)
    all_to_all x1, blocking collectives, tiled_body(): lax.all_to_all(partial_terms, EVERY, split_axis=0, concat_axis=0, tiled=T...  14.3 us
    all_to_all x1, blocking collectives, tiled_body(): lax.all_to_all(attended.reshape((-1,) + attended.shape[2:]), ('hi', 'narr...  12.4 us
    pallas_call x4, Pallas kernels, load(): pl.pallas_call(functools.partial(load_kernel, first), out_shape=pltpu.VME...  9.39 us
    ppermute x3, starting transfers between devices, tiled_body(): other = lax.ppermute(held, WIDE, [(i, i ^ step) for i in range(count)])  7.26 us
    pallas_call x1, Pallas kernels, second_product(): pl.pallas_call(second_product_kernel, out_shape=(half, half), in_specs=[W...  6.4 us
    pallas_call x1, Pallas kernels, first_product(): pl.pallas_call(first_product_kernel, out_shape=jax.ShapeDtypeStruct((rows...  4.37 us
    ppermute x1, waiting for transfers between devices, tiled_body(): lax.ppermute(send, 'narrow', [(0, 1), (1, 0)])  3.5 us
    pallas_call x1, Pallas kernels, attention(): pl.pallas_call(attention_kernel, out_shape=jax.ShapeDtypeStruct((copies,...  2.07 us
  transfers between devices with their start and end apart: 6, of which 3 were waited for; matrix products, arithmetic and copies ran while one was open for 0% of the time, Pallas kernels for 15%

profile of v3, /device:TPU:0, one launch (start us, length us, event | category | flops | bytes accessed | tf_op | source)
XLA Modules:
  0.0 64.4 jit_solution(4586758606886918470)
XLA Ops:
  0.0 4.1 %collective-permute-start = (bf16[2,8192]{1,0:T(2,128)(2,1)}, bf16[2,8192]{1,0:T(2,128)(2,1)S(1)}, u32[]{:S(2)}, u32[]{:S(2)}) collective-permute-start(bf16[2,8192]{1,0:T(2,128)(2,1)} %own_ref.1), channel_id=1, source_target_pairs={{0,16},{2,18},{4,20},{6,22},{8,24},{10,26},{12,28},{14,30},{16,0},... | collective-permute-start | bytes 98312 | tf_op jit(solution)/shard_map/ppermute | solution.py:504
  4.7 0.0 copy-start.2
  4.7 2.2 %load.4._.refs_0_ = bf16[2048,1024]{1,0:T(8,128)(2,1)S(1)} custom-call(bf16[8192,1024]{1,0:T(8,128)(2,1)} %weight_ref.6), custom_call_target="tpu_custom_call" | custom-call | bytes 4194304 | tf_op jit(solution)/shard_map/load/pallas_call | solution.py:273
  6.9 0.0 collective-permute-done.other_ref
  6.9 0.0 copy-done.2
  7.0 0.1 opening.1
  7.1 1.6 %collective-permute-start.1 = (bf16[4,64,128]{2,1,0:T(8,128)(2,1)S(1)}, bf16[4,64,128]{2,1,0:T(8,128)(2,1)S(1)}, u32[]{:S(2)}, u32[]{:S(2)}) collective-permute-start(bf16[4,64,128]{2,1,0:T(8,128)(2,1)S(1)} %get-tuple-element.11.refs_0_.a_ref), channel_id=1, source_target_pairs={{0,8},{2,10},{4,12},{6,14},{8,0},{10,2},{12,4},{14,6},{16,24},{18,... | collective-permute-start | bytes 196616 | tf_op jit(solution)/shard_map/ppermute | solution.py:504
  8.7 2.8 %load.5._.refs_1_ = bf16[3072,1024]{1,0:T(8,128)(2,1)S(1)} custom-call(bf16[8192,1024]{1,0:T(8,128)(2,1)} %weight_ref.6, bf16[4,64,128]{2,1,0:T(8,128)(2,1)S(1)} %get-tuple-element.11.refs_0_.a_ref), custom_call_target="tpu_custom_call" | custom-call | bytes 6291456 | tf_op jit(solution)/shard_map/load/pallas_call | solution.py:273
  11.5 0.0 collective-permute-done.1.b_ref
  11.6 1.6 %collective-permute-start.2 = (bf16[8,64,128]{2,1,0:T(8,128)(2,1)S(1)}, bf16[8,64,128]{2,1,0:T(8,128)(2,1)S(1)}, u32[]{:S(2)}, u32[]{:S(2)}) collective-permute-start(bf16[8,64,128]{2,1,0:T(8,128)(2,1)S(1)} %join_rows.2.refs_0_.a_ref), channel_id=1, source_target_pairs={{0,4},{2,6},{4,0},{6,2},{8,12},{10,14},{12,8},{14,10},{16,20},{18,... | collective-permute-start | bytes 393224 | tf_op jit(solution)/shard_map/ppermute | solution.py:504
  13.1 2.8 %load.6._.refs_2_ = bf16[3072,1024]{1,0:T(8,128)(2,1)S(1)} custom-call(bf16[8192,1024]{1,0:T(8,128)(2,1)} %weight_ref.6, bf16[8,64,128]{2,1,0:T(8,128)(2,1)S(1)} %join_rows.2.refs_0_.a_ref), custom_call_target="tpu_custom_call" | custom-call | bytes 6291456 | tf_op jit(solution)/shard_map/load/pallas_call | solution.py:273
  15.9 0.7 %collective-permute-done.2.b_ref = bf16[8,64,128]{2,1,0:T(8,128)(2,1)S(1)} collective-permute-done((bf16[8,64,128]{2,1,0:T(8,128)(2,1)S(1)}, bf16[8,64,128]{2,1,0:T(8,128)(2,1)S(1)}, u32[]{:S(2)}, u32[]{:S(2)}) %collective-permute-start.2) | collective-permute-done | bytes 131104 | tf_op jit(solution)/shard_map/ppermute | solution.py:504
  16.6 0.1 collective-permute-start.3
  16.7 1.6 %load.7.refs_3_ = bf16[8192,128]{1,0:T(8,128)(2,1)S(1)} custom-call(bf16[8192,128]{1,0:T(8,128)(2,1)} %weight_ref.7, bf16[16,64,128]{2,1,0:T(8,128)(2,1)S(1)} %join_rows.3.refs_0_.own_ref), custom_call_target="tpu_custom_call" | custom-call | bytes 2097152 | tf_op jit(solution)/shard_map/load/pallas_call | solution.py:273
  18.3 0.0 copy-start
  18.3 0.0 copy-start.1
  18.3 0.0 copy-start.3
  18.3 0.0 collective-permute-done.3.other_ref
  18.3 4.4 %first_product.1 = f32[32,1,1152]{2,1,0:T(1,128)S(1)} custom-call(bf16[16,64,128]{2,1,0:T(8,128)(2,1)S(1)} %join_rows.3.refs_0_.own_ref, bf16[16,64,128]{2,1,0:T(8,128)(2,1)S(1)} %collective-permute-done.3.other_ref, bf16[2048,1024]{1,0:T(8,128)(2,1)S(1)} %load.4._.refs_0_, bf16[3072,1024]{1,0:T(8,128)(2,1)S(1)} %load.5._.refs_1_, ...), custom_call_target="tpu_custom_call" | custom-call | flops 603979776 | bytes 19398656 | tf_op jit(solution)/shard_map/first_product/pallas_call | solution.py:338
  22.7 14.3 %all_to_all.10.got_ref = f32[32,1,1152]{2,1,0:T(1,128)S(1)} all-to-all(f32[32,1,1152]{2,1,0:T(1,128)S(1)} %first_product.1), channel_id=1, replica_groups=mesh['hi'=8,'lo'=2,'narrow'=2] {'hi','lo','narrow'}, dimensions={0} | all-to-all | bytes 294912 | tf_op jit(solution)/shard_map/all_to_all | solution.py:515
  37.0 0.0 copy-done
  37.0 0.0 copy-done.1
  37.0 0.0 copy-done.3
  37.0 2.1 %attention.1 = bf16[8,2,64,128]{3,2,1,0:T(8,128)(2,1)S(1)} custom-call(s32[1,128]{1,0:T(1,128)S(1)} %get-tuple-element.10.length_ref, f32[32,1,1152]{2,1,0:T(1,128)S(1)} %all_to_all.10.got_ref, bf16[1,256,1024]{2,1,0:T(8,128)(2,1)S(1)} %copy-done, bf16[1,256,1024]{2,1,0:T(8,128)(2,1)S(1)} %copy-done.1, f32[1,1024]{1,0:T(1,128)S(1)} %copy-done.3, ...), custom_call_target="tpu_custom_call" | custom-call | flops 16777216 | bytes 1048576 | tf_op jit(solution)/shard_map/attention/pallas_call | solution.py:461
  39.1 12.4 %all_to_all.11.own_ref = bf16[16,64,128]{2,1,0:T(8,128)(2,1)S(1)} all-to-all(bf16[16,64,128]{2,1,0:T(8,128)(2,1)S(1)} %bitcast.1), channel_id=1, replica_groups=mesh['hi'=8,'lo'=2,'narrow'=2] {'hi','narrow'}, dimensions={0} | all-to-all | bytes 524288 | tf_op jit(solution)/shard_map/all_to_all | solution.py:526
  51.5 0.0 collective-permute-start.4
  51.5 1.5 %collective-permute-done.4.other_ref = bf16[16,64,128]{2,1,0:T(8,128)(2,1)S(1)} collective-permute-done((bf16[16,64,128]{2,1,0:T(8,128)(2,1)S(1)}, bf16[16,64,128]{2,1,0:T(8,128)(2,1)S(1)}, u32[]{:S(2)}, u32[]{:S(2)}) %collective-permute-start.4) | collective-permute-done | bytes 262176 | tf_op jit(solution)/shard_map/ppermute | solution.py:533
  53.0 6.4 %second_product.1 = (f32[16,1024]{1,0:T(8,128)S(1)}, f32[16,1024]{1,0:T(8,128)S(1)}) custom-call(bf16[16,64,128]{2,1,0:T(8,128)(2,1)S(1)} %all_to_all.11.own_ref, bf16[16,64,128]{2,1,0:T(8,128)(2,1)S(1)} %collective-permute-done.4.other_ref, bf16[8192,1024]{1,0:T(8,128)(2,1)} %w_ref.1), custom_call_target="tpu_custom_call" | custom-call | flops 536870912 | bytes 17301504 | tf_op jit(solution)/shard_map/second_product/pallas_call | solution.py:388
  59.4 0.8 %collective-permute-start.5 = (f32[16,1024]{1,0:T(8,128)S(1)}, f32[16,1024]{1,0:T(8,128)S(1)}, u32[]{:S(2)}, u32[]{:S(2)}) collective-permute-start(f32[16,1024]{1,0:T(8,128)S(1)} %get-tuple-element.14), channel_id=1, source_target_pairs={{0,1},{1,0},{2,3},{3,2},{4,5},{5,4},{6,7},{7,6},{8,9},{9,8},{10,11... | collective-permute-start | bytes 196616 | tf_op jit(solution)/shard_map/ppermute | solution.py:535
  60.3 3.5 %collective-permute-done.5 = f32[16,1024]{1,0:T(8,128)S(1)} collective-permute-done((f32[16,1024]{1,0:T(8,128)S(1)}, f32[16,1024]{1,0:T(8,128)S(1)}, u32[]{:S(2)}, u32[]{:S(2)}) %collective-permute-start.5) | collective-permute-done | bytes 65568 | tf_op jit(solution)/shard_map/ppermute | solution.py:535
  63.8 0.6 add_convert_fusion
  (2 shorter events, 0.0 us)
Async XLA Ops:
  0.0 6.9 %collective-permute-start = (bf16[2,8192]{1,0:T(2,128)(2,1)}, bf16[2,8192]{1,0:T(2,128)(2,1)S(1)}, u32[]{:S(2)}, u32[]{:S(2)}) collective-permute-start(bf16[2,8192]{1,0:T(2,128)(2,1)} %own_ref.1), channel_id=1, source_target_pairs={{0,16},{2,18},{4,20},{6,22},{8,24},{10,26},{12,28},{14,30},{16,0},... | collective-permute-start | bytes 98312 | tf_op jit(solution)/shard_map/ppermute | solution.py:504
  4.7 2.2 %copy-start.2 = (bf16[2,8192]{1,0:T(2,128)(2,1)S(1)}, bf16[2,8192]{1,0:T(2,128)(2,1)}, u32[]{:S(2)}) copy-start(bf16[2,8192]{1,0:T(2,128)(2,1)} %own_ref.1) | copy-start | bytes 98308
  7.1 4.4 %collective-permute-start.1 = (bf16[4,64,128]{2,1,0:T(8,128)(2,1)S(1)}, bf16[4,64,128]{2,1,0:T(8,128)(2,1)S(1)}, u32[]{:S(2)}, u32[]{:S(2)}) collective-permute-start(bf16[4,64,128]{2,1,0:T(8,128)(2,1)S(1)} %get-tuple-element.11.refs_0_.a_ref), channel_id=1, source_target_pairs={{0,8},{2,10},{4,12},{6,14},{8,0},{10,2},{12,4},{14,6},{16,24},{18,... | collective-permute-start | bytes 196616 | tf_op jit(solution)/shard_map/ppermute | solution.py:504
  11.6 5.0 %collective-permute-start.2 = (bf16[8,64,128]{2,1,0:T(8,128)(2,1)S(1)}, bf16[8,64,128]{2,1,0:T(8,128)(2,1)S(1)}, u32[]{:S(2)}, u32[]{:S(2)}) collective-permute-start(bf16[8,64,128]{2,1,0:T(8,128)(2,1)S(1)} %join_rows.2.refs_0_.a_ref), channel_id=1, source_target_pairs={{0,4},{2,6},{4,0},{6,2},{8,12},{10,14},{12,8},{14,10},{16,20},{18,... | collective-permute-start | bytes 393224 | tf_op jit(solution)/shard_map/ppermute | solution.py:504
  16.6 1.7 %collective-permute-start.3 = (bf16[16,64,128]{2,1,0:T(8,128)(2,1)S(1)}, bf16[16,64,128]{2,1,0:T(8,128)(2,1)S(1)}, u32[]{:S(2)}, u32[]{:S(2)}) collective-permute-start(bf16[16,64,128]{2,1,0:T(8,128)(2,1)S(1)} %join_rows.3.refs_0_.own_ref), channel_id=1, source_target_pairs={{0,2},{2,0},{4,6},{6,4},{8,10},{10,8},{12,14},{14,12},{16,18},{18,... | collective-permute-start | bytes 786440 | tf_op jit(solution)/shard_map/ppermute | solution.py:512
  18.3 18.7 %copy-start = (bf16[1,256,1024]{2,1,0:T(8,128)(2,1)S(1)}, bf16[1,256,1024]{2,1,0:T(8,128)(2,1)}, u32[]{:S(2)}) copy-start(bf16[1,256,1024]{2,1,0:T(8,128)(2,1)} %keys_ref.1) | copy-start | bytes 1572868
  18.3 18.7 %copy-start.1 = (bf16[1,256,1024]{2,1,0:T(8,128)(2,1)S(1)}, bf16[1,256,1024]{2,1,0:T(8,128)(2,1)}, u32[]{:S(2)}) copy-start(bf16[1,256,1024]{2,1,0:T(8,128)(2,1)} %values_ref.1) | copy-start | bytes 1572868
  18.3 18.7 %copy-start.3 = (f32[1,1024]{1,0:T(1,128)S(1)}, f32[1,1024]{1,0:T(1,128)}, u32[]{:S(2)}) copy-start(f32[1,1024]{1,0:T(1,128)} %scale_ref.1) | copy-start | bytes 12292
  51.5 1.5 %collective-permute-start.4 = (bf16[16,64,128]{2,1,0:T(8,128)(2,1)S(1)}, bf16[16,64,128]{2,1,0:T(8,128)(2,1)S(1)}, u32[]{:S(2)}, u32[]{:S(2)}) collective-permute-start(bf16[16,64,128]{2,1,0:T(8,128)(2,1)S(1)} %all_to_all.11.own_ref), channel_id=1, source_target_pairs={{0,2},{2,0},{1,3},{3,1},{4,6},{6,4},{5,7},{7,5},{8,10},{10,8},{9,1... | collective-permute-start | bytes 786440 | tf_op jit(solution)/shard_map/ppermute | solution.py:533
  59.4 4.3 %collective-permute-start.5 = (f32[16,1024]{1,0:T(8,128)S(1)}, f32[16,1024]{1,0:T(8,128)S(1)}, u32[]{:S(2)}, u32[]{:S(2)}) collective-permute-start(f32[16,1024]{1,0:T(8,128)S(1)} %get-tuple-element.14), channel_id=1, source_target_pairs={{0,1},{1,0},{2,3},{3,2},{4,5},{5,4},{6,7},{7,6},{8,9},{9,8},{10,11... | collective-permute-start | bytes 196616 | tf_op jit(solution)/shard_map/ppermute | solution.py:535

commit v4 on v3

--- a/solution.py
+++ b/solution.py
@@ -351,13 +351,15 @@
     )(own, other, *weights)
 
 
-def second_product_kernel(own_ref, other_ref, w_ref, keep_ref, send_ref, turned, w_buf, sems):
+def second_product_kernel(own_ref, other_ref, w_ref, *refs):
+    *parts, keep_ref, send_ref, turned, w_buf, sems = refs
     low = lax.axis_index("lo")
     mine = lax.axis_index("narrow")
     chunks = w_buf.shape[0]
     deep = w_buf.shape[1]
+    base = sum(part.shape[0] for part in parts)
     copies = [
-        pltpu.make_async_copy(w_ref.at[pl.ds(c * deep, deep)], w_buf.at[c], sems.at[c])
+        pltpu.make_async_copy(w_ref.at[pl.ds(base + c * deep, deep)], w_buf.at[c], sems.at[c])
         for c in range(chunks)
     ]
     for copy in copies:
@@ -367,10 +369,14 @@
     tiles = own_ref.shape[1]
     place_rows(own_ref, turned, pair, 0, lambda j: 2 * j + low)
     place_rows(other_ref, turned, pair, 0, lambda j: 2 * j + (1 - low))
-    group = deep // LANES
     total = jnp.zeros((rows, w_ref.shape[1]), jnp.float32)
+    at = 0
+    for part in parts:
+        x = turned_rows(turned, rows, tiles, at // LANES, part.shape[0] // LANES)
+        total = total + jnp.dot(x, part[...], preferred_element_type=jnp.float32)
+        at += part.shape[0]
     for c in range(chunks):
-        x = turned_rows(turned, rows, tiles, c * group, group)
+        x = turned_rows(turned, rows, tiles, (at + c * deep) // LANES, deep // LANES)
         copies[c].wait()
         total = total + jnp.dot(x, w_buf[c], preferred_element_type=jnp.float32)
     half = rows // 2
@@ -379,20 +385,22 @@
     send_ref[...] = jnp.where(lower, total[half:], total[:half])
 
 
-def second_product(own, other, weight):
+def second_product(own, other, weight, parts):
     rows = 2 * own.shape[0]
     cols = weight.shape[1]
-    chunks = 8
+    deep = 512
+    chunks = (weight.shape[0] - sum(part.shape[0] for part in parts)) // deep
     weight = pltpu.with_memory_space_constraint(weight, pltpu.HBM)
+    parts = [pltpu.with_memory_space_constraint(part, pltpu.VMEM) for part in parts]
     half = jax.ShapeDtypeStruct((rows // 2, cols), jnp.float32)
     return pl.pallas_call(
         second_product_kernel,
         out_shape=(half, half),
-        in_specs=[WHOLE, WHOLE, pl.BlockSpec(memory_space=pltpu.HBM)],
+        in_specs=[WHOLE, WHOLE, pl.BlockSpec(memory_space=pltpu.HBM)] + [WHOLE] * len(parts),
         out_specs=(WHOLE, WHOLE),
         scratch_shapes=[
             pltpu.VMEM((rows * own.shape[1], LANES), jnp.float32),
-            pltpu.VMEM((chunks, weight.shape[0] // chunks, cols), weight.dtype),
+            pltpu.VMEM((chunks, deep, cols), weight.dtype),
             pltpu.SemaphoreType.DMA((chunks,)),
         ],
         compiler_params=params(24),
@@ -400,10 +408,14 @@
             flops=2 * rows * weight.size, bytes_accessed=4 * own.size + 2 * weight.size, transcendentals=0
         ),
         name="second_product",
-    )(own, other, weight)
-
-
-def attention_kernel(length_ref, got_ref, keys_ref, values_ref, scale_ref, turn_ref, o_ref):
+    )(own, other, weight, *parts)
+
+
+def attention_kernel(
+    length_ref, got_ref, keys_ref, values_ref, scale_ref, turn_ref, w_ref, o_ref, w_part_ref, sem
+):
+    ahead = pltpu.make_async_copy(w_ref.at[pl.ds(0, w_part_ref.shape[0])], w_part_ref, sem)
+    ahead.start()
     copies, parts, per_part, _ = o_ref.shape
     heads_of = (got_ref.shape[2] - LANES) // LANES
     group = QUERY_HEADS // KEY_VALUE_HEADS
@@ -453,16 +465,22 @@
         part, at = divmod(g * group, per_part)
         for copy in range(copies):
             o_ref[copy, part, at : at + group, :] = attended
-
-
-def attention(got, keys, values, scale, lengths, turn, copies, parts):
+    ahead.wait()
+
+
+def attention(got, keys, values, scale, lengths, turn, out_weight, ahead, copies, parts):
+    out_weight = pltpu.with_memory_space_constraint(out_weight, pltpu.HBM)
     keys = pltpu.with_memory_space_constraint(keys, pltpu.VMEM)
     values = pltpu.with_memory_space_constraint(values, pltpu.VMEM)
     return pl.pallas_call(
         attention_kernel,
-        out_shape=jax.ShapeDtypeStruct((copies, parts, QUERY_HEADS // parts, HEAD_SIZE), jnp.bfloat16),
-        in_specs=[WHOLE] * 6,
-        out_specs=WHOLE,
+        out_shape=(
+            jax.ShapeDtypeStruct((copies, parts, QUERY_HEADS // parts, HEAD_SIZE), jnp.bfloat16),
+            pltpu.VMEM((ahead, out_weight.shape[1]), out_weight.dtype),
+        ),
+        in_specs=[WHOLE] * 6 + [pl.BlockSpec(memory_space=pltpu.HBM)],
+        out_specs=(WHOLE, WHOLE),
+        scratch_shapes=[pltpu.SemaphoreType.DMA],
         compiler_params=params(8),
         cost_estimate=pl.CostEstimate(
             flops=4 * QUERY_HEADS * keys.shape[1] * HEAD_SIZE,
@@ -470,7 +488,7 @@
             transcendentals=QUERY_HEADS * keys.shape[1],
         ),
         name="attention",
-    )(lengths, got, keys, values, scale, turn)
+    )(lengths, got, keys, values, scale, turn, out_weight)
 
 
 def fits(tokens, q_weight, key_value_weight, stored_keys):
@@ -513,13 +531,16 @@
     kv_part = load(key_value_weight, 0, key_value_weight.shape[0], held)
     partial_terms = first_product(held, other, q_parts, kv_part)
     got = lax.all_to_all(partial_terms, EVERY, split_axis=0, concat_axis=0, tiled=True)
-    attended = attention(
+    ahead = 1536
+    attended, first_part = attention(
         got,
         stored_keys,
         stored_values,
         channel_key_scale,
         lengths,
         turn,
+        out_weight,
+        ahead,
         lax.axis_size("hi"),
         narrow,
     )
@@ -531,7 +552,8 @@
         tiled=True,
     )
     other = lax.ppermute(mine, "lo", [(0, 1), (1, 0)])
-    keep, send = second_product(mine, other, out_weight)
+    second_part = load(out_weight, ahead, 1024, mine)
+    keep, send = second_product(mine, other, out_weight, (first_part, second_part))
     return (keep + lax.ppermute(send, "narrow", [(0, 1), (1, 0)])).astype(jnp.bfloat16)
 
 

time: 64.7 us -> 63.5 us (0.981)
  waiting for transfers between devices: 5.72 us -> 4.42 us
    pallas_call x4 -> x5, Pallas kernels: 9.39 us -> 11 us  [load(): pl.pallas_call(functools.partial(load_kernel, first), out_shape=pltpu.VME...]
    pallas_call x1, Pallas kernels: 6.4 us -> 4.83 us  [second_product(): pl.pallas_call(second_product_kernel, out_shape=(half, half), in_specs=[W...]
    ppermute x1, waiting for transfers between devices: 1.53 us -> 0.01 us  [tiled_body(): other = lax.ppermute(mine, 'lo', [(0, 1), (1, 0)])]
  transfers between devices with their start and end apart: 6 -> 6, of which waited for: 3 -> 2; matrix products, arithmetic and copies ran while one was open for 0% -> 0% of each run, Pallas kernels for 15% -> 17%
where the time goes in v4:
time: 63.5 us; the launch traced here: 63.2 us
  blocking collectives  26.7 us (42%)
  Pallas kernels  22.4 us (35%)
  starting transfers between devices  8.17 us (13%)
  waiting for transfers between devices  4.42 us (7%)
  between operations  0.82 us (1%)
    all_to_all x1, blocking collectives, tiled_body(): lax.all_to_all(partial_terms, EVERY, split_axis=0, concat_axis=0, tiled=T...  14.3 us
    all_to_all x1, blocking collectives, tiled_body(): lax.all_to_all(attended.reshape((-1,) + attended.shape[2:]), ('hi', 'narr...  12.4 us
    pallas_call x5, Pallas kernels, load(): pl.pallas_call(functools.partial(load_kernel, first), out_shape=pltpu.VME...  11 us
    ppermute x3, starting transfers between devices, tiled_body(): other = lax.ppermute(held, WIDE, [(i, i ^ step) for i in range(count)])  7.26 us
    pallas_call x1, Pallas kernels, second_product(): pl.pallas_call(second_product_kernel, out_shape=(half, half), in_specs=[W...  4.83 us
    pallas_call x1, Pallas kernels, first_product(): pl.pallas_call(first_product_kernel, out_shape=jax.ShapeDtypeStruct((rows...  4.37 us
    ppermute x1, waiting for transfers between devices, tiled_body(): lax.ppermute(send, 'narrow', [(0, 1), (1, 0)])  3.74 us
    pallas_call x1, Pallas kernels, attention(): pl.pallas_call(attention_kernel, out_shape=(jax.ShapeDtypeStruct((copies,...  2.09 us
  transfers between devices with their start and end apart: 6, of which 2 were waited for; matrix products, arithmetic and copies ran while one was open for 0% of the time, Pallas kernels for 17%

profile of v4, /device:TPU:0, one launch (start us, length us, event | category | flops | bytes accessed | tf_op | source)
XLA Modules:
  0.0 63.2 jit_solution(15464480351719116247)
XLA Ops:
  0.0 4.1 %collective-permute-start = (bf16[2,8192]{1,0:T(2,128)(2,1)}, bf16[2,8192]{1,0:T(2,128)(2,1)S(1)}, u32[]{:S(2)}, u32[]{:S(2)}) collective-permute-start(bf16[2,8192]{1,0:T(2,128)(2,1)} %own_ref.1), channel_id=1, source_target_pairs={{0,16},{2,18},{4,20},{6,22},{8,24},{10,26},{12,28},{14,30},{16,0},... | collective-permute-start | bytes 98312 | tf_op jit(solution)/shard_map/ppermute | solution.py:522
  4.7 0.0 copy-start.2
  4.7 2.2 %load.5._.refs_0_ = bf16[2048,1024]{1,0:T(8,128)(2,1)S(1)} custom-call(bf16[8192,1024]{1,0:T(8,128)(2,1)} %weight_ref.7), custom_call_target="tpu_custom_call" | custom-call | bytes 4194304 | tf_op jit(solution)/shard_map/load/pallas_call | solution.py:273
  6.9 0.0 collective-permute-done.other_ref
  6.9 0.0 copy-done.2
  7.0 0.1 opening.1
  7.1 1.6 %collective-permute-start.1 = (bf16[4,64,128]{2,1,0:T(8,128)(2,1)S(1)}, bf16[4,64,128]{2,1,0:T(8,128)(2,1)S(1)}, u32[]{:S(2)}, u32[]{:S(2)}) collective-permute-start(bf16[4,64,128]{2,1,0:T(8,128)(2,1)S(1)} %get-tuple-element.13.refs_0_.a_ref), channel_id=1, source_target_pairs={{0,8},{2,10},{4,12},{6,14},{8,0},{10,2},{12,4},{14,6},{16,24},{18,... | collective-permute-start | bytes 196616 | tf_op jit(solution)/shard_map/ppermute | solution.py:522
  8.7 2.8 %load.6._.refs_1_ = bf16[3072,1024]{1,0:T(8,128)(2,1)S(1)} custom-call(bf16[8192,1024]{1,0:T(8,128)(2,1)} %weight_ref.7, bf16[4,64,128]{2,1,0:T(8,128)(2,1)S(1)} %get-tuple-element.13.refs_0_.a_ref), custom_call_target="tpu_custom_call" | custom-call | bytes 6291456 | tf_op jit(solution)/shard_map/load/pallas_call | solution.py:273
  11.5 0.0 collective-permute-done.1.b_ref
  11.6 1.6 %collective-permute-start.2 = (bf16[8,64,128]{2,1,0:T(8,128)(2,1)S(1)}, bf16[8,64,128]{2,1,0:T(8,128)(2,1)S(1)}, u32[]{:S(2)}, u32[]{:S(2)}) collective-permute-start(bf16[8,64,128]{2,1,0:T(8,128)(2,1)S(1)} %join_rows.2.refs_0_.a_ref), channel_id=1, source_target_pairs={{0,4},{2,6},{4,0},{6,2},{8,12},{10,14},{12,8},{14,10},{16,20},{18,... | collective-permute-start | bytes 393224 | tf_op jit(solution)/shard_map/ppermute | solution.py:522
  13.1 2.8 %load.7._.refs_2_ = bf16[3072,1024]{1,0:T(8,128)(2,1)S(1)} custom-call(bf16[8192,1024]{1,0:T(8,128)(2,1)} %weight_ref.7, bf16[8,64,128]{2,1,0:T(8,128)(2,1)S(1)} %join_rows.2.refs_0_.a_ref), custom_call_target="tpu_custom_call" | custom-call | bytes 6291456 | tf_op jit(solution)/shard_map/load/pallas_call | solution.py:273
  15.9 0.7 %collective-permute-done.2.b_ref = bf16[8,64,128]{2,1,0:T(8,128)(2,1)S(1)} collective-permute-done((bf16[8,64,128]{2,1,0:T(8,128)(2,1)S(1)}, bf16[8,64,128]{2,1,0:T(8,128)(2,1)S(1)}, u32[]{:S(2)}, u32[]{:S(2)}) %collective-permute-start.2) | collective-permute-done | bytes 131104 | tf_op jit(solution)/shard_map/ppermute | solution.py:522
  16.6 0.1 collective-permute-start.3
  16.7 1.6 %load.8.refs_3_ = bf16[8192,128]{1,0:T(8,128)(2,1)S(1)} custom-call(bf16[8192,128]{1,0:T(8,128)(2,1)} %weight_ref.8, bf16[16,64,128]{2,1,0:T(8,128)(2,1)S(1)} %join_rows.3.refs_0_.own_ref), custom_call_target="tpu_custom_call" | custom-call | bytes 2097152 | tf_op jit(solution)/shard_map/load/pallas_call | solution.py:273
  18.3 0.0 copy-start
  18.3 0.0 copy-start.1
  18.3 0.0 copy-start.3
  18.3 0.0 collective-permute-done.3.other_ref
  18.3 4.4 %first_product.1 = f32[32,1,1152]{2,1,0:T(1,128)S(1)} custom-call(bf16[16,64,128]{2,1,0:T(8,128)(2,1)S(1)} %join_rows.3.refs_0_.own_ref, bf16[16,64,128]{2,1,0:T(8,128)(2,1)S(1)} %collective-permute-done.3.other_ref, bf16[2048,1024]{1,0:T(8,128)(2,1)S(1)} %load.5._.refs_0_, bf16[3072,1024]{1,0:T(8,128)(2,1)S(1)} %load.6._.refs_1_, ...), custom_call_target="tpu_custom_call" | custom-call | flops 603979776 | bytes 19398656 | tf_op jit(solution)/shard_map/first_product/pallas_call | solution.py:338
  22.7 14.3 %all_to_all.10.got_ref = f32[32,1,1152]{2,1,0:T(1,128)S(1)} all-to-all(f32[32,1,1152]{2,1,0:T(1,128)S(1)} %first_product.1), channel_id=1, replica_groups=mesh['hi'=8,'lo'=2,'narrow'=2] {'hi','lo','narrow'}, dimensions={0} | all-to-all | bytes 294912 | tf_op jit(solution)/shard_map/all_to_all | solution.py:533
  37.0 0.0 copy-done
  37.0 0.0 copy-done.1
  37.0 0.0 copy-done.3
  37.0 2.1 %attention.1 = (bf16[8,2,64,128]{3,2,1,0:T(8,128)(2,1)S(1)}, bf16[1536,1024]{1,0:T(8,128)(2,1)S(1)}) custom-call(s32[1,128]{1,0:T(1,128)S(1)} %get-tuple-element.12.length_ref, f32[32,1,1152]{2,1,0:T(1,128)S(1)} %all_to_all.10.got_ref, bf16[1,256,1024]{2,1,0:T(8,128)(2,1)S(1)} %copy-done, bf16[1,256,1024]{2,1,0:T(8,128)(2,1)S(1)} %copy-done.1, ...), custom_call_target="tpu_custom_call" | custom-call | flops 16777216 | bytes 1048576 | tf_op jit(solution)/shard_map/attention/pallas_call | solution.py:475
  39.1 12.4 %all_to_all.11.refs_0_.own_ref = bf16[16,64,128]{2,1,0:T(8,128)(2,1)S(1)} all-to-all(bf16[16,64,128]{2,1,0:T(8,128)(2,1)S(1)} %bitcast.1), channel_id=1, replica_groups=mesh['hi'=8,'lo'=2,'narrow'=2] {'hi','narrow'}, dimensions={0} | all-to-all | bytes 524288 | tf_op jit(solution)/shard_map/all_to_all | solution.py:547
  51.5 0.0 collective-permute-start.4
  51.5 1.6 %load.9.refs_1_ = bf16[1024,1024]{1,0:T(8,128)(2,1)S(1)} custom-call(bf16[8192,1024]{1,0:T(8,128)(2,1)} %w_ref.3, bf16[16,64,128]{2,1,0:T(8,128)(2,1)S(1)} %all_to_all.11.refs_0_.own_ref), custom_call_target="tpu_custom_call" | custom-call | bytes 2097152 | tf_op jit(solution)/shard_map/load/pallas_call | solution.py:273
  53.2 0.0 collective-permute-done.4.other_ref
  53.2 4.8 %second_product.1 = (f32[16,1024]{1,0:T(8,128)S(1)}, f32[16,1024]{1,0:T(8,128)S(1)}) custom-call(bf16[16,64,128]{2,1,0:T(8,128)(2,1)S(1)} %all_to_all.11.refs_0_.own_ref, bf16[16,64,128]{2,1,0:T(8,128)(2,1)S(1)} %collective-permute-done.4.other_ref, bf16[8192,1024]{1,0:T(8,128)(2,1)} %w_ref.3, bf16[1536,1024]{1,0:T(8,128)(2,1)S(1)} %get-tuple-element.16.refs_0_, ...), custom_call_target="tpu_custom_call" | custom-call | flops 536870912 | bytes 17301504 | tf_op jit(solution)/shard_map/second_product/pallas_call | solution.py:396
  58.0 0.8 %collective-permute-start.5 = (f32[16,1024]{1,0:T(8,128)S(1)}, f32[16,1024]{1,0:T(8,128)S(1)}, u32[]{:S(2)}, u32[]{:S(2)}) collective-permute-start(f32[16,1024]{1,0:T(8,128)S(1)} %get-tuple-element.18), channel_id=1, source_target_pairs={{0,1},{1,0},{2,3},{3,2},{4,5},{5,4},{6,7},{7,6},{8,9},{9,8},{10,11... | collective-permute-start | bytes 196616 | tf_op jit(solution)/shard_map/ppermute | solution.py:557
  58.8 3.7 %collective-permute-done.5 = f32[16,1024]{1,0:T(8,128)S(1)} collective-permute-done((f32[16,1024]{1,0:T(8,128)S(1)}, f32[16,1024]{1,0:T(8,128)S(1)}, u32[]{:S(2)}, u32[]{:S(2)}) %collective-permute-start.5) | collective-permute-done | bytes 65568 | tf_op jit(solution)/shard_map/ppermute | solution.py:557
  62.6 0.6 add_convert_fusion
  (2 shorter events, 0.0 us)
Async XLA Ops:
  0.0 6.9 %collective-permute-start = (bf16[2,8192]{1,0:T(2,128)(2,1)}, bf16[2,8192]{1,0:T(2,128)(2,1)S(1)}, u32[]{:S(2)}, u32[]{:S(2)}) collective-permute-start(bf16[2,8192]{1,0:T(2,128)(2,1)} %own_ref.1), channel_id=1, source_target_pairs={{0,16},{2,18},{4,20},{6,22},{8,24},{10,26},{12,28},{14,30},{16,0},... | collective-permute-start | bytes 98312 | tf_op jit(solution)/shard_map/ppermute | solution.py:522
  4.7 2.2 %copy-start.2 = (bf16[2,8192]{1,0:T(2,128)(2,1)S(1)}, bf16[2,8192]{1,0:T(2,128)(2,1)}, u32[]{:S(2)}) copy-start(bf16[2,8192]{1,0:T(2,128)(2,1)} %own_ref.1) | copy-start | bytes 98308
  7.1 4.4 %collective-permute-start.1 = (bf16[4,64,128]{2,1,0:T(8,128)(2,1)S(1)}, bf16[4,64,128]{2,1,0:T(8,128)(2,1)S(1)}, u32[]{:S(2)}, u32[]{:S(2)}) collective-permute-start(bf16[4,64,128]{2,1,0:T(8,128)(2,1)S(1)} %get-tuple-element.13.refs_0_.a_ref), channel_id=1, source_target_pairs={{0,8},{2,10},{4,12},{6,14},{8,0},{10,2},{12,4},{14,6},{16,24},{18,... | collective-permute-start | bytes 196616 | tf_op jit(solution)/shard_map/ppermute | solution.py:522
  11.6 5.0 %collective-permute-start.2 = (bf16[8,64,128]{2,1,0:T(8,128)(2,1)S(1)}, bf16[8,64,128]{2,1,0:T(8,128)(2,1)S(1)}, u32[]{:S(2)}, u32[]{:S(2)}) collective-permute-start(bf16[8,64,128]{2,1,0:T(8,128)(2,1)S(1)} %join_rows.2.refs_0_.a_ref), channel_id=1, source_target_pairs={{0,4},{2,6},{4,0},{6,2},{8,12},{10,14},{12,8},{14,10},{16,20},{18,... | collective-permute-start | bytes 393224 | tf_op jit(solution)/shard_map/ppermute | solution.py:522
  16.6 1.7 %collective-permute-start.3 = (bf16[16,64,128]{2,1,0:T(8,128)(2,1)S(1)}, bf16[16,64,128]{2,1,0:T(8,128)(2,1)S(1)}, u32[]{:S(2)}, u32[]{:S(2)}) collective-permute-start(bf16[16,64,128]{2,1,0:T(8,128)(2,1)S(1)} %join_rows.3.refs_0_.own_ref), channel_id=1, source_target_pairs={{0,2},{2,0},{4,6},{6,4},{8,10},{10,8},{12,14},{14,12},{16,18},{18,... | collective-permute-start | bytes 786440 | tf_op jit(solution)/shard_map/ppermute | solution.py:530
  18.3 18.7 %copy-start = (bf16[1,256,1024]{2,1,0:T(8,128)(2,1)S(1)}, bf16[1,256,1024]{2,1,0:T(8,128)(2,1)}, u32[]{:S(2)}) copy-start(bf16[1,256,1024]{2,1,0:T(8,128)(2,1)} %keys_ref.1) | copy-start | bytes 1572868
  18.3 18.7 %copy-start.1 = (bf16[1,256,1024]{2,1,0:T(8,128)(2,1)S(1)}, bf16[1,256,1024]{2,1,0:T(8,128)(2,1)}, u32[]{:S(2)}) copy-start(bf16[1,256,1024]{2,1,0:T(8,128)(2,1)} %values_ref.1) | copy-start | bytes 1572868
  18.3 18.7 %copy-start.3 = (f32[1,1024]{1,0:T(1,128)S(1)}, f32[1,1024]{1,0:T(1,128)}, u32[]{:S(2)}) copy-start(f32[1,1024]{1,0:T(1,128)} %scale_ref.1) | copy-start | bytes 12292
  51.5 1.6 %collective-permute-start.4 = (bf16[16,64,128]{2,1,0:T(8,128)(2,1)S(1)}, bf16[16,64,128]{2,1,0:T(8,128)(2,1)S(1)}, u32[]{:S(2)}, u32[]{:S(2)}) collective-permute-start(bf16[16,64,128]{2,1,0:T(8,128)(2,1)S(1)} %all_to_all.11.refs_0_.own_ref), channel_id=1, source_target_pairs={{0,2},{2,0},{1,3},{3,1},{4,6},{6,4},{5,7},{7,5},{8,10},{10,8},{9,1... | collective-permute-start | bytes 786440 | tf_op jit(solution)/shard_map/ppermute | solution.py:554
  58.0 4.6 %collective-permute-start.5 = (f32[16,1024]{1,0:T(8,128)S(1)}, f32[16,1024]{1,0:T(8,128)S(1)}, u32[]{:S(2)}, u32[]{:S(2)}) collective-permute-start(f32[16,1024]{1,0:T(8,128)S(1)} %get-tuple-element.18), channel_id=1, source_target_pairs={{0,1},{1,0},{2,3},{3,2},{4,5},{5,4},{6,7},{7,6},{8,9},{9,8},{10,11... | collective-permute-start | bytes 196616 | tf_op jit(solution)/shard_map/ppermute | solution.py:557

commit v5 on v4

--- a/solution.py
+++ b/solution.py
@@ -285,8 +285,10 @@
     )(weight, *after)
 
 
-def first_product_kernel(own_ref, other_ref, *refs):
-    *q_refs, kv_ref, o_ref, turned = refs
+def first_product_kernel(own_ref, other_ref, w_ref, *refs):
+    *q_refs, kv_ref, o_ref, w_part_ref, turned, sem = refs
+    ahead = pltpu.make_async_copy(w_ref.at[pl.ds(0, w_part_ref.shape[0])], w_part_ref, sem)
+    ahead.start()
     me = lax.axis_index(WIDE)
     pair = 2
     rows = 2 * own_ref.shape[0]
@@ -328,19 +330,27 @@
     for r in range(rows):
         o_ref[r, :, :q_cols] = q_total[r : r + 1]
         o_ref[r, :, q_cols:] = kv_total[r : r + 1]
-
-
-def first_product(own, other, q_parts, kv_weight):
+    ahead.wait()
+
+
+def first_product(own, other, q_parts, kv_weight, out_weight, ahead):
+    out_weight = pltpu.with_memory_space_constraint(out_weight, pltpu.HBM)
     rows = 2 * own.shape[0]
     depth = kv_weight.shape[0]
     width = q_parts[0].shape[1] + kv_weight.shape[1]
     weights = [pltpu.with_memory_space_constraint(w, pltpu.VMEM) for w in (*q_parts, kv_weight)]
     return pl.pallas_call(
         first_product_kernel,
-        out_shape=jax.ShapeDtypeStruct((rows, 1, width), jnp.float32),
-        in_specs=[WHOLE] * (2 + len(weights)),
-        out_specs=WHOLE,
-        scratch_shapes=[pltpu.VMEM((rows * own.shape[1], LANES), jnp.float32)],
+        out_shape=(
+            jax.ShapeDtypeStruct((rows, 1, width), jnp.float32),
+            pltpu.VMEM((ahead, out_weight.shape[1]), out_weight.dtype),
+        ),
+        in_specs=[WHOLE, WHOLE, pl.BlockSpec(memory_space=pltpu.HBM)] + [WHOLE] * len(weights),
+        out_specs=(WHOLE, WHOLE),
+        scratch_shapes=[
+            pltpu.VMEM((rows * own.shape[1], LANES), jnp.float32),
+            pltpu.SemaphoreType.DMA,
+        ],
         compiler_params=params(6),
         cost_estimate=pl.CostEstimate(
             flops=2 * rows * depth * width,
@@ -348,7 +358,7 @@
             transcendentals=0,
         ),
         name="first_product",
-    )(own, other, *weights)
+    )(own, other, out_weight, *weights)
 
 
 def second_product_kernel(own_ref, other_ref, w_ref, *refs):
@@ -412,9 +422,19 @@
 
 
 def attention_kernel(
-    length_ref, got_ref, keys_ref, values_ref, scale_ref, turn_ref, w_ref, o_ref, w_part_ref, sem
+    first,
+    length_ref,
+    got_ref,
+    keys_ref,
+    values_ref,
+    scale_ref,
+    turn_ref,
+    w_ref,
+    o_ref,
+    w_part_ref,
+    sem,
 ):
-    ahead = pltpu.make_async_copy(w_ref.at[pl.ds(0, w_part_ref.shape[0])], w_part_ref, sem)
+    ahead = pltpu.make_async_copy(w_ref.at[pl.ds(first, w_part_ref.shape[0])], w_part_ref, sem)
     ahead.start()
     copies, parts, per_part, _ = o_ref.shape
     heads_of = (got_ref.shape[2] - LANES) // LANES
@@ -432,48 +452,71 @@
     def rotate(x):
         return x * cosine + pltpu.roll(x, HEAD_SIZE // 2, 1) * sine
 
-    live = lax.broadcasted_iota(jnp.int32, (group, slots), 1) < jnp.concatenate(
+    live = lax.broadcasted_iota(jnp.int32, (2 * group, slots), 1) < jnp.concatenate(
         [length_ref[...]] * (slots // LANES), axis=1
     )
-    for g in range(KEY_VALUE_HEADS):
-        span = slice(g * HEAD_SIZE, (g + 1) * HEAD_SIZE)
-        rows = []
-        for w in range(g * sources, (g + 1) * sources):
-            rows.append(rounded(w, 0, q_cols).reshape(heads_of, LANES))
-        rotated = rotate(jnp.concatenate(rows, axis=0))
-        fresh_key = rotate(rounded(g, q_cols, LANES)).astype(jnp.bfloat16).astype(jnp.float32)
-        fresh_value = rounded(KEY_VALUE_HEADS + g, q_cols, LANES)
-        cache_query = (rotated * scale_ref[:, span] * inverse_scale).astype(jnp.bfloat16)
-        fresh_query = (rotated * inverse_scale).astype(jnp.bfloat16).astype(jnp.float32)
+    none = jnp.zeros((group, HEAD_SIZE), jnp.bfloat16)
+    pairs = range(0, KEY_VALUE_HEADS, 2)
+    scored = []
+    for pair in pairs:
+        cache, fresh, fresh_values = [], [], []
+        for g in (pair, pair + 1):
+            rows = [
+                rounded(w, 0, q_cols).reshape(heads_of, LANES)
+                for w in range(g * sources, (g + 1) * sources)
+            ]
+            rotated = rotate(jnp.concatenate(rows, axis=0))
+            fresh_key = rotate(rounded(g, q_cols, LANES)).astype(jnp.bfloat16).astype(jnp.float32)
+            scale = scale_ref[:, g * HEAD_SIZE : (g + 1) * HEAD_SIZE]
+            cache.append((rotated * scale * inverse_scale).astype(jnp.bfloat16))
+            fresh_query = (rotated * inverse_scale).astype(jnp.bfloat16).astype(jnp.float32)
+            fresh.append(jnp.sum(fresh_query * fresh_key, axis=-1, keepdims=True))
+            fresh_values.append(
+                jnp.broadcast_to(rounded(KEY_VALUE_HEADS + g, q_cols, LANES), (group, HEAD_SIZE))
+            )
+        queries = jnp.concatenate(
+            [
+                jnp.concatenate([cache[0], none], axis=1),
+                jnp.concatenate([none, cache[1]], axis=1),
+            ],
+            axis=0,
+        )
+        span = slice(pair * HEAD_SIZE, (pair + 2) * HEAD_SIZE)
         scores = lax.dot_general(
-            cache_query,
+            queries,
             keys_ref[0, :, span],
             (((1,), (1,)), ((), ())),
             preferred_element_type=jnp.float32,
         )
-        fresh_score = jnp.sum(fresh_query * fresh_key, axis=-1, keepdims=True)
+        scored.append((scores, jnp.concatenate(fresh, axis=0), fresh_values))
+    for pair, (scores, fresh_score, fresh_values) in zip(pairs, scored, strict=True):
         masked = jnp.where(live, scores, jnp.float32(-1e30))
         top = jnp.maximum(jnp.max(masked, axis=-1, keepdims=True), fresh_score)
         exps = jnp.where(live, jnp.exp(masked - top), jnp.float32(0.0))
         fresh_exp = jnp.exp(fresh_score - top)
         total = jnp.sum(exps, axis=-1, keepdims=True) + fresh_exp
-        summed = jnp.dot(
+        span = slice(pair * HEAD_SIZE, (pair + 2) * HEAD_SIZE)
+        both = jnp.dot(
             exps.astype(jnp.bfloat16), values_ref[0, :, span], preferred_element_type=jnp.float32
         )
-        summed = summed + fresh_exp.astype(jnp.bfloat16).astype(jnp.float32) * fresh_value
+        summed = jnp.concatenate([both[:group, :HEAD_SIZE], both[group:, HEAD_SIZE:]], axis=0)
+        fresh_weight = fresh_exp.astype(jnp.bfloat16).astype(jnp.float32)
+        summed = summed + fresh_weight * jnp.concatenate(fresh_values, axis=0)
         attended = (summed / total).astype(jnp.bfloat16)
-        part, at = divmod(g * group, per_part)
+        part, at = divmod(pair * group, per_part)
         for copy in range(copies):
-            o_ref[copy, part, at : at + group, :] = attended
+            o_ref[copy, part, at : at + 2 * group, :] = attended
     ahead.wait()
 
 
-def attention(got, keys, values, scale, lengths, turn, out_weight, ahead, copies, parts):
+def attention(
+    got, keys, values, scale, lengths, turn, out_weight, first, ahead, copies, parts
+):
     out_weight = pltpu.with_memory_space_constraint(out_weight, pltpu.HBM)
     keys = pltpu.with_memory_space_constraint(keys, pltpu.VMEM)
     values = pltpu.with_memory_space_constraint(values, pltpu.VMEM)
     return pl.pallas_call(
-        attention_kernel,
+        functools.partial(attention_kernel, first),
         out_shape=(
             jax.ShapeDtypeStruct((copies, parts, QUERY_HEADS // parts, HEAD_SIZE), jnp.bfloat16),
             pltpu.VMEM((ahead, out_weight.shape[1]), out_weight.dtype),
@@ -529,10 +572,10 @@
         held_rows = [held]
     other = lax.ppermute(held, WIDE, [(i, i ^ 1) for i in range(count)])
     kv_part = load(key_value_weight, 0, key_value_weight.shape[0], held)
-    partial_terms = first_product(held, other, q_parts, kv_part)
+    ahead, next_rows, last_rows = 1280, 256, 1024
+    partial_terms, first_part = first_product(held, other, q_parts, kv_part, out_weight, ahead)
     got = lax.all_to_all(partial_terms, EVERY, split_axis=0, concat_axis=0, tiled=True)
-    ahead = 1536
-    attended, first_part = attention(
+    attended, next_part = attention(
         got,
         stored_keys,
         stored_values,
@@ -541,6 +584,7 @@
         turn,
         out_weight,
         ahead,
+        next_rows,
         lax.axis_size("hi"),
         narrow,
     )
@@ -552,8 +596,8 @@
         tiled=True,
     )
     other = lax.ppermute(mine, "lo", [(0, 1), (1, 0)])
-    second_part = load(out_weight, ahead, 1024, mine)
-    keep, send = second_product(mine, other, out_weight, (first_part, second_part))
+    last_part = load(out_weight, ahead + next_rows, last_rows, mine)
+    keep, send = second_product(mine, other, out_weight, (first_part, next_part, last_part))
     return (keep + lax.ppermute(send, "narrow", [(0, 1), (1, 0)])).astype(jnp.bfloat16)
 
 

time: 63.5 us -> 63 us (level)
    pallas_call x2, Pallas kernels: 6.46 us -> 5.44 us  [the longest x1 4.38 us: first_product(): pl.pallas_call(first_product_kernel, out_shape=(jax.ShapeDtypeStruct((row...]
  transfers between devices with their start and end apart: 6 -> 6, of which waited for: 2 -> 2; matrix products, arithmetic and copies ran while one was open for 0% -> 0% of each run, Pallas kernels for 17% -> 18%
where the time goes in v5:
time: 63 us; the launch traced here: 62.6 us
  blocking collectives  26.7 us (42%)
  Pallas kernels  21.9 us (35%)
  starting transfers between devices  8.17 us (13%)
  waiting for transfers between devices  4.42 us (7%)
  between operations  0.82 us (1%)
    all_to_all x1, blocking collectives, tiled_body(): lax.all_to_all(partial_terms, EVERY, split_axis=0, concat_axis=0, tiled=T...  14.3 us
    all_to_all x1, blocking collectives, tiled_body(): lax.all_to_all(attended.reshape((-1,) + attended.shape[2:]), ('hi', 'narr...  12.4 us
    pallas_call x5, Pallas kernels, load(): pl.pallas_call(functools.partial(load_kernel, first), out_shape=pltpu.VME...  11 us
    ppermute x3, starting transfers between devices, tiled_body(): other = lax.ppermute(held, WIDE, [(i, i ^ step) for i in range(count)])  7.26 us
    pallas_call x1, Pallas kernels, second_product(): pl.pallas_call(second_product_kernel, out_shape=(half, half), in_specs=[W...  5.3 us
    pallas_call x1, Pallas kernels, first_product(): pl.pallas_call(first_product_kernel, out_shape=(jax.ShapeDtypeStruct((row...  4.38 us
    ppermute x1, waiting for transfers between devices, tiled_body(): lax.ppermute(send, 'narrow', [(0, 1), (1, 0)])  3.74 us
  transfers between devices with their start and end apart: 6, of which 2 were waited for; matrix products, arithmetic and copies ran while one was open for 0% of the time, Pallas kernels for 18%

profile of v5, /device:TPU:0, one launch (start us, length us, event | category | flops | bytes accessed | tf_op | source)
XLA Modules:
  0.0 62.6 jit_solution(16832326580129545905)
XLA Ops:
  0.0 4.1 %collective-permute-start = (bf16[2,8192]{1,0:T(2,128)(2,1)}, bf16[2,8192]{1,0:T(2,128)(2,1)S(1)}, u32[]{:S(2)}, u32[]{:S(2)}) collective-permute-start(bf16[2,8192]{1,0:T(2,128)(2,1)} %own_ref.1), channel_id=1, source_target_pairs={{0,16},{2,18},{4,20},{6,22},{8,24},{10,26},{12,28},{14,30},{16,0},... | collective-permute-start | bytes 98312 | tf_op jit(solution)/shard_map/ppermute | solution.py:565
  4.7 0.0 copy-start.2
  4.7 2.2 %load.5._.refs_0_ = bf16[2048,1024]{1,0:T(8,128)(2,1)S(1)} custom-call(bf16[8192,1024]{1,0:T(8,128)(2,1)} %weight_ref.7), custom_call_target="tpu_custom_call" | custom-call | bytes 4194304 | tf_op jit(solution)/shard_map/load/pallas_call | solution.py:273
  6.9 0.0 collective-permute-done.other_ref
  6.9 0.0 copy-done.2
  7.0 0.1 opening.1
  7.1 1.6 %collective-permute-start.1 = (bf16[4,64,128]{2,1,0:T(8,128)(2,1)S(1)}, bf16[4,64,128]{2,1,0:T(8,128)(2,1)S(1)}, u32[]{:S(2)}, u32[]{:S(2)}) collective-permute-start(bf16[4,64,128]{2,1,0:T(8,128)(2,1)S(1)} %get-tuple-element.15.refs_0_.a_ref), channel_id=1, source_target_pairs={{0,8},{2,10},{4,12},{6,14},{8,0},{10,2},{12,4},{14,6},{16,24},{18,... | collective-permute-start | bytes 196616 | tf_op jit(solution)/shard_map/ppermute | solution.py:565
  8.7 2.8 %load.6._.refs_1_ = bf16[3072,1024]{1,0:T(8,128)(2,1)S(1)} custom-call(bf16[8192,1024]{1,0:T(8,128)(2,1)} %weight_ref.7, bf16[4,64,128]{2,1,0:T(8,128)(2,1)S(1)} %get-tuple-element.15.refs_0_.a_ref), custom_call_target="tpu_custom_call" | custom-call | bytes 6291456 | tf_op jit(solution)/shard_map/load/pallas_call | solution.py:273
  11.5 0.0 collective-permute-done.1.b_ref
  11.6 1.6 %collective-permute-start.2 = (bf16[8,64,128]{2,1,0:T(8,128)(2,1)S(1)}, bf16[8,64,128]{2,1,0:T(8,128)(2,1)S(1)}, u32[]{:S(2)}, u32[]{:S(2)}) collective-permute-start(bf16[8,64,128]{2,1,0:T(8,128)(2,1)S(1)} %join_rows.2.refs_0_.a_ref), channel_id=1, source_target_pairs={{0,4},{2,6},{4,0},{6,2},{8,12},{10,14},{12,8},{14,10},{16,20},{18,... | collective-permute-start | bytes 393224 | tf_op jit(solution)/shard_map/ppermute | solution.py:565
  13.1 2.8 %load.7._.refs_2_ = bf16[3072,1024]{1,0:T(8,128)(2,1)S(1)} custom-call(bf16[8192,1024]{1,0:T(8,128)(2,1)} %weight_ref.7, bf16[8,64,128]{2,1,0:T(8,128)(2,1)S(1)} %join_rows.2.refs_0_.a_ref), custom_call_target="tpu_custom_call" | custom-call | bytes 6291456 | tf_op jit(solution)/shard_map/load/pallas_call | solution.py:273
  15.9 0.7 %collective-permute-done.2.b_ref = bf16[8,64,128]{2,1,0:T(8,128)(2,1)S(1)} collective-permute-done((bf16[8,64,128]{2,1,0:T(8,128)(2,1)S(1)}, bf16[8,64,128]{2,1,0:T(8,128)(2,1)S(1)}, u32[]{:S(2)}, u32[]{:S(2)}) %collective-permute-start.2) | collective-permute-done | bytes 131104 | tf_op jit(solution)/shard_map/ppermute | solution.py:565
  16.6 0.1 collective-permute-start.3
  16.7 1.6 %load.8.refs_3_ = bf16[8192,128]{1,0:T(8,128)(2,1)S(1)} custom-call(bf16[8192,128]{1,0:T(8,128)(2,1)} %weight_ref.8, bf16[16,64,128]{2,1,0:T(8,128)(2,1)S(1)} %join_rows.3.refs_0_.own_ref), custom_call_target="tpu_custom_call" | custom-call | bytes 2097152 | tf_op jit(solution)/shard_map/load/pallas_call | solution.py:273
  18.3 0.0 copy-start
  18.3 0.0 copy-start.1
  18.3 0.0 copy-start.3
  18.3 0.0 collective-permute-done.3.other_ref
  18.3 4.4 %first_product.1 = (f32[32,1,1152]{2,1,0:T(1,128)S(1)}, bf16[1280,1024]{1,0:T(8,128)(2,1)S(1)}) custom-call(bf16[16,64,128]{2,1,0:T(8,128)(2,1)S(1)} %join_rows.3.refs_0_.own_ref, bf16[16,64,128]{2,1,0:T(8,128)(2,1)S(1)} %collective-permute-done.3.other_ref, bf16[8192,1024]{1,0:T(8,128)(2,1)} %w_ref.5, bf16[2048,1024]{1,0:T(8,128)(2,1)S(1)} %load.5._.refs_0_, ...), custom_call_target="tpu_custom_call" | custom-call | flops 603979776 | bytes 19398656 | tf_op jit(solution)/shard_map/first_product/pallas_call | solution.py:342
  22.7 14.3 %all_to_all.10.got_ref = f32[32,1,1152]{2,1,0:T(1,128)S(1)} all-to-all(f32[32,1,1152]{2,1,0:T(1,128)S(1)} %get-tuple-element.16), channel_id=1, replica_groups=mesh['hi'=8,'lo'=2,'narrow'=2] {'hi','lo','narrow'}, dimensions={0} | all-to-all | bytes 294912 | tf_op jit(solution)/shard_map/all_to_all | solution.py:577
  37.0 0.0 copy-done
  37.0 0.0 copy-done.1
  37.0 0.0 copy-done.3
  37.0 1.1 %attention.1 = (bf16[8,2,64,128]{3,2,1,0:T(8,128)(2,1)S(1)}, bf16[256,1024]{1,0:T(8,128)(2,1)S(1)}) custom-call(s32[1,128]{1,0:T(1,128)S(1)} %get-tuple-element.14.length_ref, f32[32,1,1152]{2,1,0:T(1,128)S(1)} %all_to_all.10.got_ref, bf16[1,256,1024]{2,1,0:T(8,128)(2,1)S(1)} %copy-done, bf16[1,256,1024]{2,1,0:T(8,128)(2,1)S(1)} %copy-done.1, ...), custom_call_target="tpu_custom_call" | custom-call | flops 16777216 | bytes 1048576 | tf_op jit(solution)/shard_map/attention/pallas_call | solution.py:518
  38.1 12.4 %all_to_all.11.refs_0_.own_ref = bf16[16,64,128]{2,1,0:T(8,128)(2,1)S(1)} all-to-all(bf16[16,64,128]{2,1,0:T(8,128)(2,1)S(1)} %bitcast.1), channel_id=1, replica_groups=mesh['hi'=8,'lo'=2,'narrow'=2] {'hi','narrow'}, dimensions={0} | all-to-all | bytes 524288 | tf_op jit(solution)/shard_map/all_to_all | solution.py:591
  50.5 0.0 collective-permute-start.4
  50.5 1.6 %load.9.refs_2_ = bf16[1024,1024]{1,0:T(8,128)(2,1)S(1)} custom-call(bf16[8192,1024]{1,0:T(8,128)(2,1)} %w_ref.5, bf16[16,64,128]{2,1,0:T(8,128)(2,1)S(1)} %all_to_all.11.refs_0_.own_ref), custom_call_target="tpu_custom_call" | custom-call | bytes 2097152 | tf_op jit(solution)/shard_map/load/pallas_call | solution.py:273
  52.1 0.0 collective-permute-done.4.other_ref
  52.1 5.3 %second_product.1 = (f32[16,1024]{1,0:T(8,128)S(1)}, f32[16,1024]{1,0:T(8,128)S(1)}) custom-call(bf16[16,64,128]{2,1,0:T(8,128)(2,1)S(1)} %all_to_all.11.refs_0_.own_ref, bf16[16,64,128]{2,1,0:T(8,128)(2,1)S(1)} %collective-permute-done.4.other_ref, bf16[8192,1024]{1,0:T(8,128)(2,1)} %w_ref.5, bf16[1280,1024]{1,0:T(8,128)(2,1)S(1)} %get-tuple-element.19.refs_0_, ...), custom_call_target="tpu_custom_call" | custom-call | flops 536870912 | bytes 17301504 | tf_op jit(solution)/shard_map/second_product/pallas_call | solution.py:406
  57.4 0.8 %collective-permute-start.5 = (f32[16,1024]{1,0:T(8,128)S(1)}, f32[16,1024]{1,0:T(8,128)S(1)}, u32[]{:S(2)}, u32[]{:S(2)}) collective-permute-start(f32[16,1024]{1,0:T(8,128)S(1)} %get-tuple-element.22), channel_id=1, source_target_pairs={{0,1},{1,0},{2,3},{3,2},{4,5},{5,4},{6,7},{7,6},{8,9},{9,8},{10,11... | collective-permute-start | bytes 196616 | tf_op jit(solution)/shard_map/ppermute | solution.py:601
  58.3 3.7 %collective-permute-done.5 = f32[16,1024]{1,0:T(8,128)S(1)} collective-permute-done((f32[16,1024]{1,0:T(8,128)S(1)}, f32[16,1024]{1,0:T(8,128)S(1)}, u32[]{:S(2)}, u32[]{:S(2)}) %collective-permute-start.5) | collective-permute-done | bytes 65568 | tf_op jit(solution)/shard_map/ppermute | solution.py:601
  62.0 0.6 add_convert_fusion
  (2 shorter events, 0.0 us)
Async XLA Ops:
  0.0 6.9 %collective-permute-start = (bf16[2,8192]{1,0:T(2,128)(2,1)}, bf16[2,8192]{1,0:T(2,128)(2,1)S(1)}, u32[]{:S(2)}, u32[]{:S(2)}) collective-permute-start(bf16[2,8192]{1,0:T(2,128)(2,1)} %own_ref.1), channel_id=1, source_target_pairs={{0,16},{2,18},{4,20},{6,22},{8,24},{10,26},{12,28},{14,30},{16,0},... | collective-permute-start | bytes 98312 | tf_op jit(solution)/shard_map/ppermute | solution.py:565
  4.7 2.2 %copy-start.2 = (bf16[2,8192]{1,0:T(2,128)(2,1)S(1)}, bf16[2,8192]{1,0:T(2,128)(2,1)}, u32[]{:S(2)}) copy-start(bf16[2,8192]{1,0:T(2,128)(2,1)} %own_ref.1) | copy-start | bytes 98308
  7.1 4.4 %collective-permute-start.1 = (bf16[4,64,128]{2,1,0:T(8,128)(2,1)S(1)}, bf16[4,64,128]{2,1,0:T(8,128)(2,1)S(1)}, u32[]{:S(2)}, u32[]{:S(2)}) collective-permute-start(bf16[4,64,128]{2,1,0:T(8,128)(2,1)S(1)} %get-tuple-element.15.refs_0_.a_ref), channel_id=1, source_target_pairs={{0,8},{2,10},{4,12},{6,14},{8,0},{10,2},{12,4},{14,6},{16,24},{18,... | collective-permute-start | bytes 196616 | tf_op jit(solution)/shard_map/ppermute | solution.py:565
  11.6 5.0 %collective-permute-start.2 = (bf16[8,64,128]{2,1,0:T(8,128)(2,1)S(1)}, bf16[8,64,128]{2,1,0:T(8,128)(2,1)S(1)}, u32[]{:S(2)}, u32[]{:S(2)}) collective-permute-start(bf16[8,64,128]{2,1,0:T(8,128)(2,1)S(1)} %join_rows.2.refs_0_.a_ref), channel_id=1, source_target_pairs={{0,4},{2,6},{4,0},{6,2},{8,12},{10,14},{12,8},{14,10},{16,20},{18,... | collective-permute-start | bytes 393224 | tf_op jit(solution)/shard_map/ppermute | solution.py:565
  16.6 1.7 %collective-permute-start.3 = (bf16[16,64,128]{2,1,0:T(8,128)(2,1)S(1)}, bf16[16,64,128]{2,1,0:T(8,128)(2,1)S(1)}, u32[]{:S(2)}, u32[]{:S(2)}) collective-permute-start(bf16[16,64,128]{2,1,0:T(8,128)(2,1)S(1)} %join_rows.3.refs_0_.own_ref), channel_id=1, source_target_pairs={{0,2},{2,0},{4,6},{6,4},{8,10},{10,8},{12,14},{14,12},{16,18},{18,... | collective-permute-start | bytes 786440 | tf_op jit(solution)/shard_map/ppermute | solution.py:573
  18.3 18.7 %copy-start = (bf16[1,256,1024]{2,1,0:T(8,128)(2,1)S(1)}, bf16[1,256,1024]{2,1,0:T(8,128)(2,1)}, u32[]{:S(2)}) copy-start(bf16[1,256,1024]{2,1,0:T(8,128)(2,1)} %keys_ref.1) | copy-start | bytes 1572868
  18.3 18.7 %copy-start.1 = (bf16[1,256,1024]{2,1,0:T(8,128)(2,1)S(1)}, bf16[1,256,1024]{2,1,0:T(8,128)(2,1)}, u32[]{:S(2)}) copy-start(bf16[1,256,1024]{2,1,0:T(8,128)(2,1)} %values_ref.1) | copy-start | bytes 1572868
  18.3 18.7 %copy-start.3 = (f32[1,1024]{1,0:T(1,128)S(1)}, f32[1,1024]{1,0:T(1,128)}, u32[]{:S(2)}) copy-start(f32[1,1024]{1,0:T(1,128)} %scale_ref.1) | copy-start | bytes 12292
  50.5 1.6 %collective-permute-start.4 = (bf16[16,64,128]{2,1,0:T(8,128)(2,1)S(1)}, bf16[16,64,128]{2,1,0:T(8,128)(2,1)S(1)}, u32[]{:S(2)}, u32[]{:S(2)}) collective-permute-start(bf16[16,64,128]{2,1,0:T(8,128)(2,1)S(1)} %all_to_all.11.refs_0_.own_ref), channel_id=1, source_target_pairs={{0,2},{2,0},{1,3},{3,1},{4,6},{6,4},{5,7},{7,5},{8,10},{10,8},{9,1... | collective-permute-start | bytes 786440 | tf_op jit(solution)/shard_map/ppermute | solution.py:598
  57.4 4.6 %collective-permute-start.5 = (f32[16,1024]{1,0:T(8,128)S(1)}, f32[16,1024]{1,0:T(8,128)S(1)}, u32[]{:S(2)}, u32[]{:S(2)}) collective-permute-start(f32[16,1024]{1,0:T(8,128)S(1)} %get-tuple-element.22), channel_id=1, source_target_pairs={{0,1},{1,0},{2,3},{3,2},{4,5},{5,4},{6,7},{7,6},{8,9},{9,8},{10,11... | collective-permute-start | bytes 196616 | tf_op jit(solution)/shard_map/ppermute | solution.py:601

commit v6 on v5

--- a/solution.py
+++ b/solution.py
@@ -572,7 +572,7 @@
         held_rows = [held]
     other = lax.ppermute(held, WIDE, [(i, i ^ 1) for i in range(count)])
     kv_part = load(key_value_weight, 0, key_value_weight.shape[0], held)
-    ahead, next_rows, last_rows = 1280, 256, 1024
+    ahead, next_rows, last_rows = 6144, 512, 512
     partial_terms, first_part = first_product(held, other, q_parts, kv_part, out_weight, ahead)
     got = lax.all_to_all(partial_terms, EVERY, split_axis=0, concat_axis=0, tiled=True)
     attended, next_part = attention(

time: 63 us -> 61.1 us (0.970)
  Pallas kernels: 21.9 us -> 19.9 us
    pallas_call x1, Pallas kernels: 5.3 us -> 3.23 us  [second_product(): pl.pallas_call(second_product_kernel, out_shape=(half, half), in_specs=[W...]
  transfers between devices with their start and end apart: 6 -> 6, of which waited for: 2 -> 3; matrix products, arithmetic and copies ran while one was open for 0% -> 0% of each run, Pallas kernels for 18% -> 18%
where the time goes in v6:
time: 61.1 us; the launch traced here: 60.7 us
  blocking collectives  26.7 us (44%)
  Pallas kernels  19.9 us (33%)
  starting transfers between devices  8.17 us (13%)
  waiting for transfers between devices  4.48 us (7%)
  between operations  0.81 us (1%)
  other arithmetic  0.62 us (1%)
    all_to_all x1, blocking collectives, tiled_body(): lax.all_to_all(partial_terms, EVERY, split_axis=0, concat_axis=0, tiled=T...  14.3 us
    all_to_all x1, blocking collectives, tiled_body(): lax.all_to_all(attended.reshape((-1,) + attended.shape[2:]), ('hi', 'narr...  12.4 us
    pallas_call x5, Pallas kernels, load(): pl.pallas_call(functools.partial(load_kernel, first), out_shape=pltpu.VME...  10.6 us
    ppermute x3, starting transfers between devices, tiled_body(): other = lax.ppermute(held, WIDE, [(i, i ^ step) for i in range(count)])  7.26 us
    pallas_call x1, Pallas kernels, first_product(): pl.pallas_call(first_product_kernel, out_shape=(jax.ShapeDtypeStruct((row...  4.67 us
    ppermute x1, waiting for transfers between devices, tiled_body(): lax.ppermute(send, 'narrow', [(0, 1), (1, 0)])  3.5 us
    pallas_call x1, Pallas kernels, second_product(): pl.pallas_call(second_product_kernel, out_shape=(half, half), in_specs=[W...  3.23 us
    pallas_call x1, Pallas kernels, attention(): pl.pallas_call(functools.partial(attention_kernel, first), out_shape=(jax...  1.24 us
  transfers between devices with their start and end apart: 6, of which 3 were waited for; matrix products, arithmetic and copies ran while one was open for 0% of the time, Pallas kernels for 18%

profile of v6, /device:TPU:0, one launch (start us, length us, event | category | flops | bytes accessed | tf_op | source)
XLA Modules:
  0.0 60.7 jit_solution(5545382701828224465)
XLA Ops:
  0.0 4.1 %collective-permute-start = (bf16[2,8192]{1,0:T(2,128)(2,1)}, bf16[2,8192]{1,0:T(2,128)(2,1)S(1)}, u32[]{:S(2)}, u32[]{:S(2)}) collective-permute-start(bf16[2,8192]{1,0:T(2,128)(2,1)} %own_ref.1), channel_id=1, source_target_pairs={{0,16},{2,18},{4,20},{6,22},{8,24},{10,26},{12,28},{14,30},{16,0},... | collective-permute-start | bytes 98312 | tf_op jit(solution)/shard_map/ppermute | solution.py:565
  4.7 0.0 copy-start.2
  4.7 2.2 %load.5._.refs_0_ = bf16[2048,1024]{1,0:T(8,128)(2,1)S(1)} custom-call(bf16[8192,1024]{1,0:T(8,128)(2,1)} %weight_ref.7), custom_call_target="tpu_custom_call" | custom-call | bytes 4194304 | tf_op jit(solution)/shard_map/load/pallas_call | solution.py:273
  6.9 0.0 collective-permute-done.other_ref
  6.9 0.0 copy-done.2
  7.0 0.1 opening.1
  7.1 1.6 %collective-permute-start.1 = (bf16[4,64,128]{2,1,0:T(8,128)(2,1)S(1)}, bf16[4,64,128]{2,1,0:T(8,128)(2,1)S(1)}, u32[]{:S(2)}, u32[]{:S(2)}) collective-permute-start(bf16[4,64,128]{2,1,0:T(8,128)(2,1)S(1)} %get-tuple-element.15.refs_0_.a_ref), channel_id=1, source_target_pairs={{0,8},{2,10},{4,12},{6,14},{8,0},{10,2},{12,4},{14,6},{16,24},{18,... | collective-permute-start | bytes 196616 | tf_op jit(solution)/shard_map/ppermute | solution.py:565
  8.7 2.8 %load.6._.refs_1_ = bf16[3072,1024]{1,0:T(8,128)(2,1)S(1)} custom-call(bf16[8192,1024]{1,0:T(8,128)(2,1)} %weight_ref.7, bf16[4,64,128]{2,1,0:T(8,128)(2,1)S(1)} %get-tuple-element.15.refs_0_.a_ref), custom_call_target="tpu_custom_call" | custom-call | bytes 6291456 | tf_op jit(solution)/shard_map/load/pallas_call | solution.py:273
  11.5 0.0 collective-permute-done.1.b_ref
  11.6 1.6 %collective-permute-start.2 = (bf16[8,64,128]{2,1,0:T(8,128)(2,1)S(1)}, bf16[8,64,128]{2,1,0:T(8,128)(2,1)S(1)}, u32[]{:S(2)}, u32[]{:S(2)}) collective-permute-start(bf16[8,64,128]{2,1,0:T(8,128)(2,1)S(1)} %join_rows.2.refs_0_.a_ref), channel_id=1, source_target_pairs={{0,4},{2,6},{4,0},{6,2},{8,12},{10,14},{12,8},{14,10},{16,20},{18,... | collective-permute-start | bytes 393224 | tf_op jit(solution)/shard_map/ppermute | solution.py:565
  13.1 2.8 %load.7._.refs_2_ = bf16[3072,1024]{1,0:T(8,128)(2,1)S(1)} custom-call(bf16[8192,1024]{1,0:T(8,128)(2,1)} %weight_ref.7, bf16[8,64,128]{2,1,0:T(8,128)(2,1)S(1)} %join_rows.2.refs_0_.a_ref), custom_call_target="tpu_custom_call" | custom-call | bytes 6291456 | tf_op jit(solution)/shard_map/load/pallas_call | solution.py:273
  15.9 0.7 %collective-permute-done.2.b_ref = bf16[8,64,128]{2,1,0:T(8,128)(2,1)S(1)} collective-permute-done((bf16[8,64,128]{2,1,0:T(8,128)(2,1)S(1)}, bf16[8,64,128]{2,1,0:T(8,128)(2,1)S(1)}, u32[]{:S(2)}, u32[]{:S(2)}) %collective-permute-start.2) | collective-permute-done | bytes 131104 | tf_op jit(solution)/shard_map/ppermute | solution.py:565
  16.6 0.1 collective-permute-start.3
  16.7 1.6 %load.8.refs_3_ = bf16[8192,128]{1,0:T(8,128)(2,1)S(1)} custom-call(bf16[8192,128]{1,0:T(8,128)(2,1)} %weight_ref.8, bf16[16,64,128]{2,1,0:T(8,128)(2,1)S(1)} %join_rows.3.refs_0_.own_ref), custom_call_target="tpu_custom_call" | custom-call | bytes 2097152 | tf_op jit(solution)/shard_map/load/pallas_call | solution.py:273
  18.3 0.0 copy-start
  18.3 0.0 copy-start.1
  18.3 0.0 copy-start.3
  18.3 0.0 collective-permute-done.3.other_ref
  18.3 4.7 %first_product.1 = (f32[32,1,1152]{2,1,0:T(1,128)S(1)}, bf16[6144,1024]{1,0:T(8,128)(2,1)S(1)}) custom-call(bf16[16,64,128]{2,1,0:T(8,128)(2,1)S(1)} %join_rows.3.refs_0_.own_ref, bf16[16,64,128]{2,1,0:T(8,128)(2,1)S(1)} %collective-permute-done.3.other_ref, bf16[8192,1024]{1,0:T(8,128)(2,1)} %w_ref.5, bf16[2048,1024]{1,0:T(8,128)(2,1)S(1)} %load.5._.refs_0_, ...), custom_call_target="tpu_custom_call" | custom-call | flops 603979776 | bytes 19398656 | tf_op jit(solution)/shard_map/first_product/pallas_call | solution.py:342
  23.0 14.3 %all_to_all.10.got_ref = f32[32,1,1152]{2,1,0:T(1,128)S(1)} all-to-all(f32[32,1,1152]{2,1,0:T(1,128)S(1)} %get-tuple-element.16), channel_id=1, replica_groups=mesh['hi'=8,'lo'=2,'narrow'=2] {'hi','lo','narrow'}, dimensions={0} | all-to-all | bytes 294912 | tf_op jit(solution)/shard_map/all_to_all | solution.py:577
  37.3 0.0 copy-done
  37.3 0.0 copy-done.1
  37.3 0.0 copy-done.3
  37.3 1.2 %attention.1 = (bf16[8,2,64,128]{3,2,1,0:T(8,128)(2,1)S(1)}, bf16[512,1024]{1,0:T(8,128)(2,1)S(1)}) custom-call(s32[1,128]{1,0:T(1,128)S(1)} %get-tuple-element.14.length_ref, f32[32,1,1152]{2,1,0:T(1,128)S(1)} %all_to_all.10.got_ref, bf16[1,256,1024]{2,1,0:T(8,128)(2,1)S(1)} %copy-done, bf16[1,256,1024]{2,1,0:T(8,128)(2,1)S(1)} %copy-done.1, ...), custom_call_target="tpu_custom_call" | custom-call | flops 16777216 | bytes 1048576 | tf_op jit(solution)/shard_map/attention/pallas_call | solution.py:518
  38.5 12.4 %all_to_all.11.refs_0_.own_ref = bf16[16,64,128]{2,1,0:T(8,128)(2,1)S(1)} all-to-all(bf16[16,64,128]{2,1,0:T(8,128)(2,1)S(1)} %bitcast.1), channel_id=1, replica_groups=mesh['hi'=8,'lo'=2,'narrow'=2] {'hi','narrow'}, dimensions={0} | all-to-all | bytes 524288 | tf_op jit(solution)/shard_map/all_to_all | solution.py:591
  51.0 0.0 collective-permute-start.4
  51.0 1.2 %load.9.refs_2_ = bf16[512,1024]{1,0:T(8,128)(2,1)S(1)} custom-call(bf16[8192,1024]{1,0:T(8,128)(2,1)} %w_ref.5, bf16[16,64,128]{2,1,0:T(8,128)(2,1)S(1)} %all_to_all.11.refs_0_.own_ref), custom_call_target="tpu_custom_call" | custom-call | bytes 1048576 | tf_op jit(solution)/shard_map/load/pallas_call | solution.py:273
  52.2 0.3 collective-permute-done.4.other_ref
  52.5 3.2 %second_product.1 = (f32[16,1024]{1,0:T(8,128)S(1)}, f32[16,1024]{1,0:T(8,128)S(1)}) custom-call(bf16[16,64,128]{2,1,0:T(8,128)(2,1)S(1)} %all_to_all.11.refs_0_.own_ref, bf16[16,64,128]{2,1,0:T(8,128)(2,1)S(1)} %collective-permute-done.4.other_ref, bf16[8192,1024]{1,0:T(8,128)(2,1)} %w_ref.5, bf16[6144,1024]{1,0:T(8,128)(2,1)S(1)} %get-tuple-element.19.refs_0_, ...), custom_call_target="tpu_custom_call" | custom-call | flops 536870912 | bytes 17301504 | tf_op jit(solution)/shard_map/second_product/pallas_call | solution.py:406
  55.8 0.8 %collective-permute-start.5 = (f32[16,1024]{1,0:T(8,128)S(1)}, f32[16,1024]{1,0:T(8,128)S(1)}, u32[]{:S(2)}, u32[]{:S(2)}) collective-permute-start(f32[16,1024]{1,0:T(8,128)S(1)} %get-tuple-element.22), channel_id=1, source_target_pairs={{0,1},{1,0},{2,3},{3,2},{4,5},{5,4},{6,7},{7,6},{8,9},{9,8},{10,11... | collective-permute-start | bytes 196616 | tf_op jit(solution)/shard_map/ppermute | solution.py:601
  56.6 3.5 %collective-permute-done.5 = f32[16,1024]{1,0:T(8,128)S(1)} collective-permute-done((f32[16,1024]{1,0:T(8,128)S(1)}, f32[16,1024]{1,0:T(8,128)S(1)}, u32[]{:S(2)}, u32[]{:S(2)}) %collective-permute-start.5) | collective-permute-done | bytes 65568 | tf_op jit(solution)/shard_map/ppermute | solution.py:601
  60.1 0.6 %add_convert_fusion = bf16[16,1024]{1,0:T(8,128)(2,1)} fusion(f32[16,1024]{1,0:T(8,128)S(1)} %get-tuple-element.21, f32[16,1024]{1,0:T(8,128)S(1)} %collective-permute-done.5), kind=kLoop, calls=%fused_computation | loop fusion | flops 32768 | bytes 163840 | tf_op jit(solution)/shard_map/convert_element_type | solution.py:601
  (2 shorter events, 0.0 us)
Async XLA Ops:
  0.0 6.9 %collective-permute-start = (bf16[2,8192]{1,0:T(2,128)(2,1)}, bf16[2,8192]{1,0:T(2,128)(2,1)S(1)}, u32[]{:S(2)}, u32[]{:S(2)}) collective-permute-start(bf16[2,8192]{1,0:T(2,128)(2,1)} %own_ref.1), channel_id=1, source_target_pairs={{0,16},{2,18},{4,20},{6,22},{8,24},{10,26},{12,28},{14,30},{16,0},... | collective-permute-start | bytes 98312 | tf_op jit(solution)/shard_map/ppermute | solution.py:565
  4.7 2.2 %copy-start.2 = (bf16[2,8192]{1,0:T(2,128)(2,1)S(1)}, bf16[2,8192]{1,0:T(2,128)(2,1)}, u32[]{:S(2)}) copy-start(bf16[2,8192]{1,0:T(2,128)(2,1)} %own_ref.1) | copy-start | bytes 98308
  7.1 4.4 %collective-permute-start.1 = (bf16[4,64,128]{2,1,0:T(8,128)(2,1)S(1)}, bf16[4,64,128]{2,1,0:T(8,128)(2,1)S(1)}, u32[]{:S(2)}, u32[]{:S(2)}) collective-permute-start(bf16[4,64,128]{2,1,0:T(8,128)(2,1)S(1)} %get-tuple-element.15.refs_0_.a_ref), channel_id=1, source_target_pairs={{0,8},{2,10},{4,12},{6,14},{8,0},{10,2},{12,4},{14,6},{16,24},{18,... | collective-permute-start | bytes 196616 | tf_op jit(solution)/shard_map/ppermute | solution.py:565
  11.6 5.0 %collective-permute-start.2 = (bf16[8,64,128]{2,1,0:T(8,128)(2,1)S(1)}, bf16[8,64,128]{2,1,0:T(8,128)(2,1)S(1)}, u32[]{:S(2)}, u32[]{:S(2)}) collective-permute-start(bf16[8,64,128]{2,1,0:T(8,128)(2,1)S(1)} %join_rows.2.refs_0_.a_ref), channel_id=1, source_target_pairs={{0,4},{2,6},{4,0},{6,2},{8,12},{10,14},{12,8},{14,10},{16,20},{18,... | collective-permute-start | bytes 393224 | tf_op jit(solution)/shard_map/ppermute | solution.py:565
  16.6 1.7 %collective-permute-start.3 = (bf16[16,64,128]{2,1,0:T(8,128)(2,1)S(1)}, bf16[16,64,128]{2,1,0:T(8,128)(2,1)S(1)}, u32[]{:S(2)}, u32[]{:S(2)}) collective-permute-start(bf16[16,64,128]{2,1,0:T(8,128)(2,1)S(1)} %join_rows.3.refs_0_.own_ref), channel_id=1, source_target_pairs={{0,2},{2,0},{4,6},{6,4},{8,10},{10,8},{12,14},{14,12},{16,18},{18,... | collective-permute-start | bytes 786440 | tf_op jit(solution)/shard_map/ppermute | solution.py:573
  18.3 19.0 %copy-start = (bf16[1,256,1024]{2,1,0:T(8,128)(2,1)S(1)}, bf16[1,256,1024]{2,1,0:T(8,128)(2,1)}, u32[]{:S(2)}) copy-start(bf16[1,256,1024]{2,1,0:T(8,128)(2,1)} %keys_ref.1) | copy-start | bytes 1572868
  18.3 19.0 %copy-start.1 = (bf16[1,256,1024]{2,1,0:T(8,128)(2,1)S(1)}, bf16[1,256,1024]{2,1,0:T(8,128)(2,1)}, u32[]{:S(2)}) copy-start(bf16[1,256,1024]{2,1,0:T(8,128)(2,1)} %values_ref.1) | copy-start | bytes 1572868
  18.3 19.0 %copy-start.3 = (f32[1,1024]{1,0:T(1,128)S(1)}, f32[1,1024]{1,0:T(1,128)}, u32[]{:S(2)}) copy-start(f32[1,1024]{1,0:T(1,128)} %scale_ref.1) | copy-start | bytes 12292
  51.0 1.5 %collective-permute-start.4 = (bf16[16,64,128]{2,1,0:T(8,128)(2,1)S(1)}, bf16[16,64,128]{2,1,0:T(8,128)(2,1)S(1)}, u32[]{:S(2)}, u32[]{:S(2)}) collective-permute-start(bf16[16,64,128]{2,1,0:T(8,128)(2,1)S(1)} %all_to_all.11.refs_0_.own_ref), channel_id=1, source_target_pairs={{0,2},{2,0},{1,3},{3,1},{4,6},{6,4},{5,7},{7,5},{8,10},{10,8},{9,1... | collective-permute-start | bytes 786440 | tf_op jit(solution)/shard_map/ppermute | solution.py:598
  55.8 4.3 %collective-permute-start.5 = (f32[16,1024]{1,0:T(8,128)S(1)}, f32[16,1024]{1,0:T(8,128)S(1)}, u32[]{:S(2)}, u32[]{:S(2)}) collective-permute-start(f32[16,1024]{1,0:T(8,128)S(1)} %get-tuple-element.22), channel_id=1, source_target_pairs={{0,1},{1,0},{2,3},{3,2},{4,5},{5,4},{6,7},{7,6},{8,9},{9,8},{10,11... | collective-permute-start | bytes 196616 | tf_op jit(solution)/shard_map/ppermute | solution.py:601
